TPU v7x, 32 devices: a whole 2x2x4 slice. The times are simulated.
32 devices in a mesh: prow: 4 (over y, core), pcol: 8 (over z, x).
Axes of the slice: x: 2, y: 2, z: 4, core: 2. Of those that a mesh axis runs over, the one named last changes fastest.
Arguments:
- matrix: bfloat16 [14336, 4096], P('prow', 'pcol'), may hold values from -6 to 6
- u_inverse: float32 [2, 512, 512], replicated, may hold values from -0.02 to 0.2, as said below
- l_inverse: float32 [2, 512, 512], replicated, may hold values from -0.02 to 0.2, as said below
Outputs:
- factored: bfloat16 [14336, 4096], P('prow', 'pcol')
Inputs may be any that keep to these rules, and one draw needn't show every extreme that they name: u_inverse[p] is upper triangular with positive diagonal. l_inverse[p] is lower triangular with positive diagonal.
All inputs are finite; a program needn't handle non-finite values.
Results may differ from a plain program's by a relative error of at most 0.008.
Values may be sent and summed in bfloat16 or wider, within the bound.
A program may use at most 64 MiB of HBM per device.

v0:
```python
import functools

import jax
import jax.numpy as jnp
from jax import lax
from jax.experimental import pallas as pl
from jax.experimental.pallas import tpu as pltpu
from jax.sharding import PartitionSpec as P

MESH = pl.DeviceIdType.MESH
BF = jnp.bfloat16
F32 = jnp.float32
PER_BLOCK = 16
PIECES = 2


def dot(a, b):
    return jnp.dot(a, b, preferred_element_type=F32)


def times_upper(a, u_ref, panel):
    half = a.shape[1] // 2
    left = sum(dot(a[:, :half], u_ref[panel, i, :half, :half]) for i in reversed(range(PIECES)))
    right = sum(dot(a, u_ref[panel, i, :, half:]) for i in reversed(range(PIECES)))
    return jnp.concatenate([left, right], 1).astype(BF)


def kernel(
    n_prow, n_pcol, width, m_ref, u_hbm, l_hbm, out_ref,
    own, buf, sbuf, uf, lf, us, ls, ucat, u1, lg1, cg1, low0, low1, cur, fresh, obuf,
    local_sem, recv, fwd, cross, sp_recv, sp_send, out_sem,
):
    rows = own.shape[0]
    chunk = width // PER_BLOCK
    chunks = rows // chunk
    half, blocks = width // 2, rows // width
    first = chunks - 4 * (2 * blocks - 1)
    prow, pcol = lax.axis_index("prow"), lax.axis_index("pcol")
    q, r = pcol % 2, prow % 2
    qx, rx = 1 - q, 1 - r
    pcol_x, prow_x = pcol + 1 - 2 * q, prow + 1 - 2 * r
    source, last = pcol < 2, pcol + 2 >= n_pcol
    top, bottom = prow < 2, prow + 2 >= n_prow
    special = pl.ds(rows, width)

    load_own = pltpu.make_async_copy(m_ref, own, local_sem.at[0])
    load_u = pltpu.make_async_copy(u_hbm, uf, local_sem.at[1])
    load_l = pltpu.make_async_copy(l_hbm, lf, local_sem.at[2])
    load_stream = pltpu.make_async_copy(m_ref, buf.at[q, pl.ds(0, rows)], local_sem.at[3])
    load_special = pltpu.make_async_copy(
        m_ref.at[pl.ds(0, width)], buf.at[q, special], local_sem.at[4]
    )
    load_head = pltpu.make_async_copy(m_ref.at[pl.ds(0, width)], sbuf.at[r], local_sem.at[5])
    source_special = source & (prow == qx)

    @pl.when(source)
    def _():
        load_stream.start()

    @pl.when(source_special)
    def _():
        load_special.start()

    @pl.when(top)
    def _():
        load_head.start()

    load_u.start()
    load_l.start()
    load_own.start()

    barrier = pltpu.get_barrier_semaphore()

    def greet(where):
        pl.semaphore_signal(barrier, inc=1, device_id=where, device_id_type=MESH)

    greet({"pcol": pcol_x})
    greet({"prow": prow_x})
    for ok, where in (
        (jnp.logical_not(source), {"pcol": pcol - 2}),
        (jnp.logical_not(last), {"pcol": pcol + 2}),
        (jnp.logical_not(top), {"prow": prow - 2}),
        (jnp.logical_not(bottom), {"prow": prow + 2}),
    ):
        pl.when(ok)(functools.partial(greet, where))
    absent = [jnp.where(ok, 1, 0) for ok in (source, last, top, bottom)]
    pl.semaphore_wait(barrier, 6 - sum(absent))

    def place(stream, k):
        shift = jnp.where((prow == 1 - stream) & (k < PER_BLOCK), rows, 0)
        at = pl.multiple_of(shift + k * chunk, chunk)
        return buf.at[stream, pl.ds(at, chunk)], (prow != stream) | (k >= PER_BLOCK)

    def stream_copy(stream, k, send_sem, where, src=None):
        ref, _ = place(stream, k)
        return pltpu.make_async_remote_copy(
            src_ref=ref if src is None else src, dst_ref=ref, send_sem=send_sem.at[k], recv_sem=recv.at[stream, k],
            device_id={"pcol": where}, device_id_type=MESH,
        )

    def send(k, src=None):
        @pl.when(jnp.logical_not(last))
        def _():
            stream_copy(q, k, fwd, pcol + 2, src).start()

        stream_copy(q, k, cross, pcol_x, src).start()

    def send_own(k):
        send(k, m_ref.at[pl.ds(pl.multiple_of(k * chunk, chunk), chunk)])

    ahead = jnp.where(prow == q, PER_BLOCK, 0)

    def relay(slot):
        k = slot + ahead

        @pl.when(jnp.logical_not(source) & (k < chunks))
        def _():
            stream_copy(q, k, fwd, pcol_x).wait_recv()
            send(k)

    def arrive(k):
        @pl.when(place(qx, k)[1])
        def _():
            stream_copy(qx, k, fwd, pcol_x).wait_recv()

    def loop(lo, hi, step):
        def one(k, carry):
            step(k)
            return carry

        lax.fori_loop(lo, hi, one, 0)

    def special_copy(which, across):
        ref = sbuf.at[r] if which == 0 else buf.at[rx, special]
        i = which + 2 * across
        return pltpu.make_async_remote_copy(
            src_ref=ref, dst_ref=ref, send_sem=sp_send.at[i], recv_sem=sp_recv.at[i],
            device_id={"prow": prow_x if across else prow + 2}, device_id_type=MESH,
        )

    def arrived_special(which, across):
        mine = rx if across else r
        ref = sbuf.at[mine] if which == 0 else buf.at[1 - mine, special]
        i = which + 2 * across
        pltpu.make_async_remote_copy(
            src_ref=ref, dst_ref=ref, send_sem=sp_send.at[i], recv_sem=sp_recv.at[i],
            device_id={"prow": prow_x}, device_id_type=MESH,
        ).wait_recv()

    def pass_special(which):
        @pl.when(jnp.logical_not(bottom))
        def _():
            special_copy(which, 0).start()

        special_copy(which, 1).start()

    @pl.when(source)
    def _():
        loop(ahead, chunks, send_own)

    @pl.when(top)
    def _():
        load_head.wait()
        pass_special(0)

    @pl.when(source_special)
    def _():
        load_special.wait()

    loop(0, 6, relay)
    pl.when(source)(load_stream.wait)
    load_u.wait()
    load_l.wait()
    load_own.wait()

    def split(src, dst, panel):
        rest = src[panel]
        for i in range(PIECES):
            piece = rest.astype(BF)
            dst[panel, i] = piece
            rest = rest - piece.astype(F32)

    for n, (src, dst, panel) in enumerate(((lf, ls, 0), (uf, us, 0), (lf, ls, 1), (uf, us, 1))):
        split(src, dst, panel)
        relay(6 + n)
    loop(10, PER_BLOCK + 2, relay)

    @pl.when(top)
    def _():
        pl.when(q == r)(functools.partial(loop, 0, PER_BLOCK, arrive))
        pass_special(1)

    loop(PER_BLOCK + 2, 2 * PER_BLOCK, relay)

    @pl.when(jnp.logical_not(top))
    def _():
        arrived_special(0, 0)
        pass_special(0)

    loop(2 * PER_BLOCK, first - 16, relay)

    @pl.when(jnp.logical_not(top))
    def _():
        arrived_special(1, 0)
        pass_special(1)

    loop(first - 16, first - 8, relay)
    arrived_special(0, 1)
    arrived_special(1, 1)

    def lower_times(panel, value, out, at, slot):
        upper = sum(dot(ls[panel, i, :half, :half], value[:half]) for i in reversed(range(PIECES)))
        out[:half, at] = upper.astype(BF)
        relay(slot)
        lower = sum(dot(ls[panel, i, half:], value) for i in reversed(range(PIECES)))
        out[half:, at] = lower.astype(BF)
        relay(slot + 1)

    whole = slice(0, width)
    lower_times(0, buf[1, special], ucat, whole, first - 8)
    lower_times(0, sbuf[0], ucat, slice(width, 2 * width), first - 6)
    lg1[...] = times_upper(buf[0, special], us, 0)
    relay(first - 4)
    cg1[...] = (sbuf[1].astype(F32) - dot(lg1[...], ucat[:, width:])).astype(BF)
    relay(first - 3)
    lower_times(1, cg1[...], u1, whole, first - 2)

    def store(at, n, value, sem):
        obuf[pl.ds(at, n)] = value
        pltpu.make_async_copy(obuf.at[pl.ds(at, n)], out_ref.at[pl.ds(at, n)], sem).start()

    @pl.when(prow == 0)
    def _():
        store(0, width, jnp.where(pcol == 0, own[:width], ucat[:, width:]), out_sem.at[0])

    @pl.when(prow == 1)
    def _():
        value = jnp.where(pcol == 1, cg1[...], u1[...])
        store(0, width, jnp.where(pcol == 0, lg1[...], value), out_sem.at[0])

    def block(at, n, sem, between, active):
        at = pl.multiple_of(at, n)
        here, part = pl.ds(at, n), pl.ds(0, n)

        @pl.when(active)
        def _():
            low0[part] = times_upper(buf[0, here], us, 0)

        between(0)

        @pl.when(active)
        def _():
            a = dot(low0[part], ucat[...])
            cur[part] = (buf[1, here].astype(F32) - a[:, :width]).astype(BF)
            fresh[part] = (own[here].astype(F32) - a[:, width:]).astype(BF)

        between(1)

        @pl.when(active)
        def _():
            low1[part] = times_upper(cur[part], us, 1)

        between(2)

        @pl.when(active)
        def _():
            value = (fresh[part].astype(F32) - dot(low1[part], u1[...])).astype(BF)
            value = jnp.where(pcol == 1, low1[part], value)
            store(at, n, jnp.where(pcol == 0, low0[part], value), sem)

        between(3)

    tiles = 2 * blocks - 1

    def one_tile(t, between):
        skip = (t < 2) & top

        @pl.when(jnp.logical_not(skip & (q == r)))
        def _():
            loop(t * (PER_BLOCK // 2), (t + 1) * (PER_BLOCK // 2), arrive)

        block(t * half, half, out_sem.at[1 + t], between, jnp.logical_not(skip))

    def nothing(slot):
        pass

    loop(0, tiles - 1, lambda t: one_tile(t, lambda slot: relay(first + 4 * t + slot)))
    loop(first + 4 * (tiles - 1), chunks, relay)
    one_tile(tiles - 1, nothing)

    quarter = half // 2

    def one_quarter(n):
        lo = tiles * (PER_BLOCK // 2) + n * (PER_BLOCK // 4)
        loop(lo, lo + PER_BLOCK // 4, arrive)
        block(lo * chunk, quarter, out_sem.at[1 + tiles + n], nothing, True)

    one_quarter(0)

    for i in range(4):
        if i < 2:
            pl.when(jnp.logical_not(bottom))(special_copy(i, 0).wait_send)
        else:
            special_copy(i - 2, 1).wait_send()

    def sent(k):
        pl.when(jnp.logical_not(last))(lambda: stream_copy(q, k, fwd, pcol_x).wait_send())
        stream_copy(q, k, cross, pcol_x).wait_send()

    late = chunks - PER_BLOCK // 2
    loop(ahead, late, sent)
    one_quarter(1)

    loop(late, chunks, sent)

    def written(at, n, sem):
        pltpu.make_async_copy(obuf.at[pl.ds(at, n)], out_ref.at[pl.ds(at, n)], sem).wait()

    pl.when(top)(lambda: written(0, width, out_sem.at[0]))
    loop(
        jnp.where(top, 2, 0),
        tiles,
        lambda t: written(pl.multiple_of(t * half, half), half, out_sem.at[1 + t]),
    )
    for n in range(2):
        written(rows - half + n * quarter, quarter, out_sem.at[1 + tiles + n])


def body(n_prow, n_pcol, matrix, u_inverse, l_inverse):
    rows, width = matrix.shape
    chunks = rows // (width // PER_BLOCK)
    square = (width, width)
    dma = pltpu.SemaphoreType.DMA
    operands = [
        pltpu.with_memory_space_constraint(x, pltpu.HBM) for x in (matrix, u_inverse, l_inverse)
    ]
    return pl.pallas_call(
        functools.partial(kernel, n_prow, n_pcol, width),
        out_shape=jax.ShapeDtypeStruct(matrix.shape, matrix.dtype),
        in_specs=[pl.BlockSpec(memory_space=pltpu.HBM)] * 3,
        out_specs=pl.BlockSpec(memory_space=pl.ANY),
        scratch_shapes=[
            pltpu.VMEM((rows, width), BF),
            pltpu.VMEM((2, rows + width, width), BF),
            pltpu.VMEM((2,) + square, BF),
            pltpu.VMEM((2,) + square, F32),
            pltpu.VMEM((2,) + square, F32),
            pltpu.VMEM((2, PIECES) + square, BF),
            pltpu.VMEM((2, PIECES) + square, BF),
            pltpu.VMEM((width, 2 * width), BF),
        ]
        + [pltpu.VMEM(square, BF)] * 7
        + [
            pltpu.VMEM((rows, width), BF),
            dma((6,)),
            dma((2, chunks)),
            dma((chunks,)),
            dma((chunks,)),
            dma((4,)),
            dma((4,)),
            dma((2 * rows // width + 2,)),
        ],
        compiler_params=pltpu.CompilerParams(
            collective_id=0, has_side_effects=True, vmem_limit_bytes=46 * 1024 * 1024
        ),
    )(*operands)


def solution(mesh):
    run = functools.partial(body, mesh.shape["prow"], mesh.shape["pcol"])
    in_specs = (P("prow", "pcol"), P(), P())
    out_specs = P("prow", "pcol")
    return jax.shard_map(run, mesh=mesh, in_specs=in_specs, out_specs=out_specs, check_vma=False)
```

profile of v0, /device:TPU:28, one launch (start us, length us, event | category | flops | bytes accessed | tf_op | source)
XLA Modules:
  0.0 97.3 jit_solution(11708628154613121217)
XLA Ops:
  0.0 95.5 %shard_map.37 = bf16[3584,512]{1,0:T(8,128)(2,1)S(1)} custom-call(bf16[3584,512]{1,0:T(8,128)(2,1)} %m_ref.1, f32[2,512,512]{2,1,0:T(8,128)} %u_hbm.1, f32[2,512,512]{2,1,0:T(8,128)} %l_hbm.1), custom_call_target="tpu_custom_call" | custom-call | tf_op jit(solution)/shard_map/pallas_call | solution.py:337
  95.5 1.8 %copy.5 = bf16[3584,512]{1,0:T(8,128)(2,1)} copy(bf16[3584,512]{1,0:T(8,128)(2,1)S(1)} %shard_map.37) | data formatting | bytes 7340032
where the time goes:
time: 97.5 us; the launch traced here: 97.3 us
  Pallas kernels  95.5 us (98%)
  local copies, waits for them, and re-layouts  1.84 us (2%)
    pallas_call x1, Pallas kernels, body(): pl.pallas_call(functools.partial(kernel, n_prow, n_pcol, width), out_shap...  95.5 us

commit v1 on v0

v1 whole, which is shorter than its diff:
```python
import functools

import jax
import jax.numpy as jnp
from jax import lax
from jax.experimental import pallas as pl
from jax.experimental.pallas import tpu as pltpu
from jax.sharding import PartitionSpec as P

MESH = pl.DeviceIdType.MESH
BF = jnp.bfloat16
F32 = jnp.float32
PIECES = 2
PER = 4


def sizes(rows, width, n_prow):
    tile = width // PER
    moved = 3 * PER // 2 if n_prow > 2 else 0
    return tile, tile // 2, tile // 4, rows // tile, moved


def dot(a, b):
    return jnp.dot(a, b, preferred_element_type=F32)


def times_upper(a, u_ref, panel):
    half = a.shape[1] // 2
    left = sum(dot(a[:, :half], u_ref[panel, i, :half, :half]) for i in reversed(range(PIECES)))
    right = sum(dot(a, u_ref[panel, i, :, half:]) for i in reversed(range(PIECES)))
    return jnp.concatenate([left, right], 1).astype(BF)


def kernel(
    n_prow, n_pcol, width, m_ref, u_hbm, l_hbm, out_ref,
    own, buf, head, uf, lf, us, ls, u0, u1,
    load_sem, recv, fwd, cross, ysem, hrecv, hsend, out_sem,
):
    rows = own.shape[0]
    tile, unit, pkt, tiles, moved = sizes(rows, width, n_prow)
    n_pkt = rows // pkt
    half = width // 2
    prow, pcol = lax.axis_index("prow"), lax.axis_index("pcol")
    x, r = pcol % 2, prow % 2
    pcol_x, prow_x = pcol + 1 - 2 * x, prow + 1 - 2 * r
    is_s0, is_s1, is_g = pcol == 0, pcol == 1, pcol >= 2
    source, last = pcol < 2, pcol + 2 >= n_pcol
    top, bottom = prow < 2, prow + 2 >= n_prow
    far = jnp.logical_not(last)
    lends, borrows = (prow == 2) & (moved > 0), (prow == 0) & (moved > 0)

    a0 = jnp.where(prow == 0, PER, 0)
    n_a = tiles - a0
    n_r = jnp.where(borrows, moved, 0)
    b0 = jnp.where(top, PER, jnp.where(lends, moved, 0))
    n_b = tiles - b0

    def at(ph, p):
        return buf.at[ph, pl.ds(pl.multiple_of(p * pkt, pkt), pkt)]

    def m_at(p):
        return m_ref.at[pl.ds(pl.multiple_of(p * pkt, pkt), pkt)]

    def own_at(p):
        return own.at[pl.ds(pl.multiple_of(p * pkt, pkt), pkt)]

    def remote(src, dst, send_sem, recv_sem, where):
        return pltpu.make_async_remote_copy(
            src_ref=src, dst_ref=dst, send_sem=send_sem, recv_sem=recv_sem,
            device_id=where, device_id_type=MESH,
        )

    def fwd_copy(ph, p, src=None):
        ref = at(ph, p)
        return remote(ref if src is None else src, ref, fwd.at[ph, p], recv.at[ph, p], {"pcol": pcol + 2})

    def cross_copy(ph, p, src=None):
        ref = at(ph, p)
        return remote(ref if src is None else src, ref, cross.at[ph, p], recv.at[ph, p], {"pcol": pcol_x})

    def raw_copy(p):
        return remote(m_at(p), own_at(p), cross.at[0, p], recv.at[1, p], {"pcol": pcol_x})

    def lent(j):
        return 2 * (2 * (j // 2) + x) + j % 2

    def lend_copy(j):
        return remote(at(1, lent(j)), at(1, n_pkt + j), ysem.at[j], recv.at[1, n_pkt + j], {"prow": prow - 2})

    def give_copy(j):
        return remote(at(1, n_pkt + j), at(1, lent(j)), ysem.at[j], recv.at[1, lent(j)], {"prow": prow + 2})

    def arrived(ph, p):
        cross_copy(ph, p).wait_recv()

    def loop(lo, hi, step):
        def one(k, carry):
            step(k)
            return carry

        lax.fori_loop(lo, hi, one, 0)

    def pair(t, lane):
        p = 2 * (2 * t + lane)
        return p, p + 1

    load_lane = pltpu.make_async_copy(m_ref, buf.at[0, pl.ds(0, rows)], load_sem.at[0])
    load_own = pltpu.make_async_copy(m_ref, own, load_sem.at[0])
    load_u = pltpu.make_async_copy(u_hbm, uf, load_sem.at[1])
    load_l = pltpu.make_async_copy(l_hbm, lf, load_sem.at[2])
    has_head = (prow == 0) & (pcol >= 1)
    load_head = pltpu.make_async_copy(m_ref.at[pl.ds(0, width)], head, load_sem.at[3])
    pl.when(has_head)(load_head.start)
    load_u.start()
    load_l.start()
    pl.when(is_s0)(load_lane.start)
    pl.when(jnp.logical_not(is_s0))(load_own.start)

    barrier = pltpu.get_barrier_semaphore()

    def greet(where):
        pl.semaphore_signal(barrier, inc=1, device_id=where, device_id_type=MESH)

    greet({"pcol": pcol_x})
    greet({"prow": prow_x})
    for ok, where in (
        (jnp.logical_not(source), {"pcol": pcol - 2}),
        (far, {"pcol": pcol + 2}),
        (jnp.logical_not(top), {"prow": prow - 2}),
        (jnp.logical_not(bottom), {"prow": prow + 2}),
    ):
        pl.when(ok)(functools.partial(greet, where))
    absent = [jnp.where(ok, 1, 0) for ok in (source, last, top, bottom)]
    pl.semaphore_wait(barrier, 6 - sum(absent))

    def head_copy(i, where, src=head):
        return remote(src, head, hsend.at[i], hrecv.at[0], where)

    def pass_head(src=head):
        head_copy(0, {"prow": prow + 1}, src).start()
        pl.when(jnp.logical_not(bottom))(lambda: head_copy(1, {"prow": prow + 2}, src).start())

    @pl.when(has_head)
    def _():
        first = m_ref.at[pl.ds(0, width)]
        pl.when(is_s1)(lambda: head_copy(2, {"pcol": pcol_x}, first).start())
        pass_head(first)

    @pl.when(is_s0)
    def _():
        def send(t):
            for p, c in zip(pair(t, 0), pair(t, 1)):
                pl.when(far)(lambda: fwd_copy(0, p, m_at(p)).start())
                cross_copy(0, c, m_at(c)).start()

        loop(a0, tiles, send)

    @pl.when(is_s1)
    def _():
        def send(t):
            for p in pair(t, 0):
                raw_copy(p).start()

        loop(a0, tiles, send)

    def split(src, dst, panel):
        rest = src[panel]
        for i in range(PIECES):
            piece = rest.astype(BF)
            dst[panel, i] = piece
            rest = rest - piece.astype(F32)

    load_u.wait()
    load_l.wait()
    split(lf, ls, 0)
    split(uf, us, 0)
    pl.when(source)(lambda: split(uf, us, 1))
    pl.when(is_g & (prow == 1))(lambda: split(lf, ls, 1))
    pl.when(is_s0)(load_lane.wait)
    pl.when(jnp.logical_not(is_s0))(load_own.wait)

    def lower_times(panel, value, out):
        upper = sum(dot(ls[panel, i, :half, :half], value[:half]) for i in reversed(range(PIECES)))
        out[:half] = upper.astype(BF)
        lower = sum(dot(ls[panel, i, half:], value) for i in reversed(range(PIECES)))
        out[half:] = lower.astype(BF)

    def first_upper():
        pl.when(has_head)(load_head.wait)

        @pl.when(jnp.logical_not(has_head))
        def _():
            head_copy(0, {"prow": prow_x}).wait_recv()
            pl.when(r == 0)(pass_head)

        lower_times(0, head[...], u0)

    def out_copy(src, at_row, n, sem):
        return pltpu.make_async_copy(src, out_ref.at[pl.ds(at_row, n)], sem)

    def out_tile(src, t):
        here = pl.ds(pl.multiple_of(t * tile, tile), tile)
        return pltpu.make_async_copy(src.at[here], out_ref.at[here], out_sem.at[t])

    def out_first(src):
        return out_copy(src, 0, width, out_sem.at[tiles])

    def make_lower(t, low, lane):
        here = pl.ds(pl.multiple_of((2 * t + lane) * unit, unit), unit)
        cur = (own[here].astype(F32) - dot(low, u0[...])).astype(BF)
        value = times_upper(cur, us, 1)
        buf[1, here] = jnp.where((prow == 1) & (t < PER), cur, value)

    def lend(t):
        @pl.when(lends & (t >= 0) & (t < moved))
        def _():
            for i in range(2):
                lend_copy(2 * t + i).start()

    def borrow():
        @pl.when(borrows)
        def _():
            def one(j):
                arrived(1, n_pkt + j)
                pl.when(far)(lambda: fwd_copy(1, n_pkt + j).start())

            loop(0, 2 * moved, one)

    def sent_common():
        pl.when(lends)(lambda: loop(0, 2 * moved, lambda j: lend_copy(j).wait_send()))
        pl.when(borrows & far)(lambda: loop(0, 2 * moved, lambda j: fwd_copy(1, n_pkt + j).wait_send()))

    @pl.when(is_s0)
    def _():
        first_upper()
        wait_raw = lambda p: remote(own_at(p), own_at(p), cross.at[1, p], recv.at[1, p], {"pcol": pcol_x}).wait_recv()
        begin = 16

        pl.when(prow == 0)(lambda: out_first(buf.at[0, pl.ds(0, width)]).start())

        def send(t):
            for p in pair(t, 0):
                pl.when(far & (t >= b0))(lambda: fwd_copy(1, p).start())
                cross_copy(1, p).start()

        def step(i):
            t = a0 + i
            here = pl.ds(pl.multiple_of(t * tile, tile), tile)
            low = times_upper(buf[0, here], us, 0)
            buf[0, here] = low
            for p in pair(t, 0):
                wait_raw(p)
            make_lower(t, low[:unit], 0)
            out_tile(buf.at[0], t).start()
            lend(t - 1)
            pl.when(i == begin)(borrow)

            @pl.when(i > begin)
            def _():
                for n in range(2):
                    send(a0 + 2 * (i - begin - 1) + n)

        loop(0, n_a, step)
        loop(a0 + 2 * (n_a - begin - 1), tiles, send)

        def sent(t):
            for p, c in zip(pair(t, 0), pair(t, 1)):
                pl.when(far)(lambda: fwd_copy(0, p).wait_send())
                cross_copy(0, c).wait_send()
                pl.when(far & (t >= b0))(lambda: fwd_copy(1, p).wait_send())
                cross_copy(1, p).wait_send()
            out_tile(buf.at[0], t).wait()

        loop(a0, tiles, sent)
        sent_common()
        pl.when(prow == 0)(lambda: out_first(buf.at[0, pl.ds(0, width)]).wait())

    @pl.when(is_s1)
    def _():
        lag = 8

        def relay(t):
            for p in pair(t, 1):
                arrived(0, p)
                pl.when(far)(lambda: fwd_copy(0, p).start())

        def make(t):
            here = pl.ds(pl.multiple_of((2 * t + 1) * unit, unit), unit)
            make_lower(t, times_upper(buf[0, here], us, 0), 1)
            lend(t - 1)

        def step(s):
            relay(a0 + s)
            pl.when(s == lag)(first_upper)
            pl.when(s >= lag)(lambda: make(a0 + s - lag))

        loop(0, n_a, step)
        pl.when(prow == 0)(lambda: out_first(u0).start())
        borrow()

        def late(i):
            pl.when(i < lag)(lambda: make(tiles - lag + i))
            for p in pair(b0 + i, 1):
                pl.when(far)(lambda: fwd_copy(1, p).start())

        loop(0, n_b, late)

        def finish(t):
            for p in pair(t, 0):
                arrived(1, p)
            out_tile(buf.at[1], t).start()

        loop(a0, tiles, finish)

        def sent(t):
            for p, c in zip(pair(t, 0), pair(t, 1)):
                raw_copy(p).wait_send()
                pl.when(far)(lambda: fwd_copy(0, c).wait_send())
                pl.when(far & (t >= b0))(lambda: fwd_copy(1, c).wait_send())
            out_tile(buf.at[1], t).wait()

        loop(a0, tiles, sent)
        sent_common()

        @pl.when(prow == 0)
        def _():
            out_first(u0).wait()
            head_copy(2, {"pcol": pcol_x}).wait_send()

    @pl.when(is_g)
    def _():
        lag_a = 4
        lag_b = jnp.where(x == 0, 4, 3)
        b_from = n_a + n_r
        total = b_from + n_b
        cross_lent = tiles
        use_lent = tiles + 6
        first_of_1 = lag_a + PER

        def u1_copy(i, where):
            return remote(u1, u1, hsend.at[3 + i], hrecv.at[1], where)

        def pass_u1():
            u1_copy(0, {"prow": prow - 1}).start()
            pl.when(jnp.logical_not(bottom))(lambda: u1_copy(1, {"prow": prow + 2}).start())

        def arrived_u1():
            u1_copy(0, {"prow": prow_x}).wait_recv()

        def apply_a(t):
            for p in pair(t, 1 - x):
                arrived(0, p)
            here = pl.ds(pl.multiple_of(t * tile, tile), tile)
            low = times_upper(buf[0, here], us, 0)
            own[here] = (own[here].astype(F32) - dot(low, u0[...])).astype(BF)

        def apply_b(t):
            for p in pair(t, 1 - x):
                arrived(1, p)
            here = pl.ds(pl.multiple_of(t * tile, tile), tile)
            own[here] = (own[here].astype(F32) - dot(buf[1, here], u1[...])).astype(BF)
            out_tile(own, t).start()

        def step(s):
            in_a = s < n_a
            in_r = jnp.logical_not(in_a) & (s < b_from)
            ph = jnp.where(in_a, 0, 1)
            p0 = jnp.where(in_a, 2 * (2 * (a0 + s) + x), 2 * (2 * (b0 + s - b_from) + x))
            p0 = jnp.where(in_r, n_pkt + 2 * (s - n_a), p0)

            def relay(i):
                @pl.when(s < total)
                def _():
                    p = p0 + i
                    arrived(ph, p)
                    pl.when(far)(lambda: fwd_copy(ph, p).start())
                    pl.when(jnp.logical_not(in_r))(lambda: cross_copy(ph, p).start())
                    pl.when(in_r)(lambda: give_copy(p - n_pkt).start())

            relay(0)
            pl.when(s == lag_a)(first_upper)
            ta = s - lag_a
            pl.when((ta >= 0) & (ta < n_a))(lambda: apply_a(a0 + ta))
            relay(1)

            @pl.when((prow == 1) & (s == first_of_1))
            def _():
                lower_times(1, own[pl.ds(0, width)], u1)

            pl.when((prow == 1) & (s == first_of_1 + 1))(pass_u1)
            pl.when((prow == 0) & (s == first_of_1 + 1))(lambda: out_first(u0).start())
            pl.when((prow == 1) & (s == first_of_1 + 1))(lambda: out_first(u1).start())

            @pl.when((r == 1) & (prow > 1) & (s == tiles - PER - 2))
            def _():
                arrived_u1()
                pass_u1()

            pl.when((r == 0) & (s == tiles - PER - 1))(arrived_u1)

            @pl.when(lends & (s >= cross_lent) & (s < cross_lent + moved))
            def _():
                for p in pair(s - cross_lent, x):
                    arrived(1, p)
                    cross_copy(1, p).start()

            tb = s - b_from - lag_b
            n_plain = jnp.where((tb >= 0) & (tb < n_b), 1, 0)
            n_lent = jnp.where(lends & (s >= use_lent) & (s < use_lent + moved), 1, 0)
            loop(
                1 - n_plain, 1 + n_lent,
                lambda k: apply_b(jnp.where(k == 0, b0 + tb, s - use_lent)),
            )

        loop(0, total + lag_b, step)

        def sent(ph, t):
            for p in pair(t, x):
                pl.when(far)(lambda: fwd_copy(ph, p).wait_send())
                cross_copy(ph, p).wait_send()

        loop(a0, tiles, lambda t: sent(0, t))
        loop(b0, tiles, lambda t: sent(1, t))

        @pl.when(borrows)
        def _():
            def one(j):
                give_copy(j).wait_send()
                pl.when(far)(lambda: fwd_copy(1, n_pkt + j).wait_send())

            loop(0, 2 * moved, one)

        @pl.when(lends)
        def _():
            def one(t):
                for p in pair(t, x):
                    cross_copy(1, p).wait_send()

            loop(0, moved, one)

        @pl.when(r == 1)
        def _():
            u1_copy(0, {"prow": prow_x}).wait_send()
            pl.when(jnp.logical_not(bottom))(lambda: u1_copy(1, {"prow": prow_x}).wait_send())

        loop(jnp.where(top, PER, 0), tiles, lambda t: out_tile(own, t).wait())
        pl.when(top)(lambda: out_first(u0).wait())

    @pl.when(r == 0)
    def _():
        head_copy(0, {"prow": prow_x}).wait_send()
        pl.when(jnp.logical_not(bottom))(lambda: head_copy(1, {"prow": prow_x}).wait_send())


def body(n_prow, n_pcol, matrix, u_inverse, l_inverse):
    rows, width = matrix.shape
    tile, unit, pkt, tiles, moved = sizes(rows, width, n_prow)
    square = (width, width)
    n_pkt = rows // pkt
    dma = pltpu.SemaphoreType.DMA
    operands = [
        pltpu.with_memory_space_constraint(a, pltpu.HBM) for a in (matrix, u_inverse, l_inverse)
    ]
    return pl.pallas_call(
        functools.partial(kernel, n_prow, n_pcol, width),
        out_shape=jax.ShapeDtypeStruct(matrix.shape, matrix.dtype),
        in_specs=[pl.BlockSpec(memory_space=pltpu.HBM)] * 3,
        out_specs=pl.BlockSpec(memory_space=pl.ANY),
        scratch_shapes=[
            pltpu.VMEM((rows, width), BF),
            pltpu.VMEM((2, rows + moved * unit, width), BF),
            pltpu.VMEM(square, BF),
            pltpu.VMEM((2,) + square, F32),
            pltpu.VMEM((2,) + square, F32),
            pltpu.VMEM((2, PIECES) + square, BF),
            pltpu.VMEM((2, PIECES) + square, BF),
            pltpu.VMEM(square, BF),
            pltpu.VMEM(square, BF),
            dma((4,)),
            dma((2, n_pkt + 2 * moved)),
            dma((2, n_pkt + 2 * moved)),
            dma((2, n_pkt)),
            dma((max(2 * moved, 1),)),
            dma((2,)),
            dma((5,)),
            dma((tiles + 1,)),
        ],
        compiler_params=pltpu.CompilerParams(
            collective_id=0, has_side_effects=True, vmem_limit_bytes=46 * 1024 * 1024
        ),
    )(*operands)


def solution(mesh):
    run = functools.partial(body, mesh.shape["prow"], mesh.shape["pcol"])
    in_specs = (P("prow", "pcol"), P(), P())
    out_specs = P("prow", "pcol")
    return jax.shard_map(run, mesh=mesh, in_specs=in_specs, out_specs=out_specs, check_vma=False)
```

time: 97.5 us -> 105 us (1.077)
  the two profiles are of different devices: /device:TPU:28 before, /device:TPU:29 now
where the time goes in v1:
time: 105 us
  Pallas kernels  103 us (98%)
  local copies, waits for them, and re-layouts  1.84 us (2%)
    pallas_call x1, Pallas kernels, body(): pl.pallas_call(functools.partial(kernel, n_prow, n_pcol, width), out_shap...  103 us

profile of v1, /device:TPU:29, one launch (start us, length us, event | category | flops | bytes accessed | tf_op | source)
XLA Modules:
  0.0 104.6 jit_solution(11471921611038066331)
XLA Ops:
  0.0 102.7 %shard_map.37 = bf16[3584,512]{1,0:T(8,128)(2,1)S(1)} custom-call(bf16[3584,512]{1,0:T(8,128)(2,1)} %m_ref.1, f32[2,512,512]{2,1,0:T(8,128)} %u_hbm.1, f32[2,512,512]{2,1,0:T(8,128)} %l_hbm.1), custom_call_target="tpu_custom_call" | custom-call | tf_op jit(solution)/shard_map/pallas_call | solution.py:464
  102.7 1.8 %copy.5 = bf16[3584,512]{1,0:T(8,128)(2,1)} copy(bf16[3584,512]{1,0:T(8,128)(2,1)S(1)} %shard_map.37) | data formatting | bytes 7340032

commit v2 on v1

v2 whole, which is shorter than its diff:
```python
import functools

import jax
import jax.numpy as jnp
from jax import lax
from jax.experimental import pallas as pl
from jax.experimental.pallas import tpu as pltpu
from jax.sharding import PartitionSpec as P

MESH = pl.DeviceIdType.MESH
BF = jnp.bfloat16
F32 = jnp.float32
PIECES = 2
PER = 4
EARLY = 8
HEAD_AT = 20


def sizes(rows, width, n_prow):
    tile = width // PER
    moved = 3 * PER // 2 if n_prow > 2 else 0
    return tile, tile // 2, tile // 4, rows // tile, moved


def dot(a, b):
    return jnp.dot(a, b, preferred_element_type=F32)


def times_upper(a, u_ref, panel):
    half = a.shape[1] // 2
    left = sum(dot(a[:, :half], u_ref[panel, i, :half, :half]) for i in reversed(range(PIECES)))
    right = sum(dot(a, u_ref[panel, i, :, half:]) for i in reversed(range(PIECES)))
    return jnp.concatenate([left, right], 1).astype(BF)


def kernel(
    n_prow, n_pcol, width, m_ref, u_hbm, l_hbm, out_ref,
    own, buf, head, uf, lf, us, ls, u0, u1,
    load_sem, lane_sem, unit_sem, send_sem, hrecv, hsend, out_sem,
):
    rows = own.shape[0]
    tile, unit, pkt, tiles, moved = sizes(rows, width, n_prow)
    n_pkt = rows // pkt
    lane_pkts = 2 * tiles
    half = width // 2
    prow, pcol = lax.axis_index("prow"), lax.axis_index("pcol")
    x, r = pcol % 2, prow % 2
    pcol_x, prow_x = pcol + 1 - 2 * x, prow + 1 - 2 * r
    is_s0, is_s1, is_g = pcol == 0, pcol == 1, pcol >= 2
    source, last = pcol < 2, pcol + 2 >= n_pcol
    top, bottom = prow < 2, prow + 2 >= n_prow
    far = jnp.logical_not(last)
    lends, borrows = (prow == 2) & (moved > 0), (prow == 0) & (moved > 0)

    a0 = jnp.where(prow == 0, PER, 0)
    n_a = tiles - a0
    n_r = jnp.where(borrows, moved, 0)
    b0 = jnp.where(top, PER, jnp.where(lends, moved, 0))
    n_b = tiles - b0

    def at(ph, p):
        return buf.at[ph, pl.ds(pl.multiple_of(p * pkt, pkt), pkt)]

    def m_at(p):
        return m_ref.at[pl.ds(pl.multiple_of(p * pkt, pkt), pkt)]

    def unit_of(t, lane):
        return pl.ds(pl.multiple_of((2 * t + lane) * unit, unit), unit)

    def tile_of(t):
        return pl.ds(pl.multiple_of(t * tile, tile), tile)

    def remote(src, dst, sem, recv_sem, where):
        return pltpu.make_async_remote_copy(
            src_ref=src, dst_ref=dst, send_sem=sem, recv_sem=recv_sem,
            device_id=where, device_id_type=MESH,
        )

    FWD, CROSS, SIDE = (send_sem.at[i] for i in range(3))

    def lane_at(ph, t, i):
        return lane_sem.at[ph * lane_pkts + 2 * t + i]

    def spare_at(j):
        return lane_sem.at[jnp.where(j < 2 * PER, j, lane_pkts + j - 2 * PER)]

    def unit_at(ph, t):
        return unit_sem.at[ph * tiles + t]

    def row_of(t, lane, i):
        return 2 * (2 * t + lane) + i

    def fwd_copy(ph, p, sem, src=None):
        ref = at(ph, p)
        return remote(ref if src is None else src, ref, FWD, sem, {"pcol": pcol + 2})

    def arrived(ph, p, sem):
        ref = at(ph, p)
        remote(ref, ref, FWD, sem, {"pcol": pcol_x}).wait_recv()

    def cross_copy(ph, t, p):
        ref = at(ph, p)
        return remote(ref, ref, CROSS, unit_at(ph, t), {"pcol": pcol_x})

    def unit_copy(ph, t, lane, dst, src=None):
        ref = dst.at[unit_of(t, lane)]
        return remote(ref if src is None else src, ref, CROSS, unit_at(ph, t), {"pcol": pcol_x})

    def lend_copy(j):
        return remote(at(1, row_of(j // 2, x, j % 2)), at(1, n_pkt + j), SIDE, spare_at(j), {"prow": prow - 2})

    def give_copy(j):
        return remote(
            at(1, n_pkt + j), at(1, row_of(j // 2, x, j % 2)), SIDE, lane_at(1, j // 2, j % 2), {"prow": prow + 2}
        )

    def sent(sem, units):
        ref = buf.at[0, pl.ds(0, units * unit)]
        remote(ref, ref, sem, lane_sem.at[0], {"pcol": pcol_x}).wait_send()

    def sent_by_prow(sem, units):
        for k, n in enumerate(units):
            here = prow == k if k + 1 < len(units) else prow >= k
            pl.when(here)(functools.partial(sent, sem, n))

    def loop(lo, hi, step):
        def one(k, carry):
            step(k)
            return carry

        lax.fori_loop(lo, hi, one, 0)

    load_lane = pltpu.make_async_copy(m_ref, buf.at[0, pl.ds(0, rows)], load_sem.at[0])
    load_own = pltpu.make_async_copy(m_ref, own, load_sem.at[0])
    load_u = pltpu.make_async_copy(u_hbm, uf, load_sem.at[1])
    load_l = pltpu.make_async_copy(l_hbm, lf, load_sem.at[2])
    has_head = (prow == 0) & (pcol >= 1)
    load_head = pltpu.make_async_copy(m_ref.at[pl.ds(0, width)], head, load_sem.at[3])
    pl.when(has_head)(load_head.start)
    load_u.start()
    load_l.start()
    pl.when(is_s0)(load_lane.start)
    pl.when(jnp.logical_not(is_s0))(load_own.start)

    barrier = pltpu.get_barrier_semaphore()

    def greet(where):
        pl.semaphore_signal(barrier, inc=1, device_id=where, device_id_type=MESH)

    greet({"pcol": pcol_x})
    greet({"prow": prow_x})
    for ok, where in (
        (jnp.logical_not(source), {"pcol": pcol - 2}),
        (far, {"pcol": pcol + 2}),
        (jnp.logical_not(top), {"prow": prow - 2}),
        (jnp.logical_not(bottom), {"prow": prow + 2}),
    ):
        pl.when(ok)(functools.partial(greet, where))
    absent = [jnp.where(ok, 1, 0) for ok in (source, last, top, bottom)]
    pl.semaphore_wait(barrier, 6 - sum(absent))

    def head_copy(i, where, src=head):
        return remote(src, head, hsend.at[i], hrecv.at[0], where)

    def pass_head(src=head):
        head_copy(0, {"prow": prow + 1}, src).start()
        pl.when(jnp.logical_not(bottom))(lambda: head_copy(1, {"prow": prow + 2}, src).start())

    @pl.when(has_head)
    def _():
        first = m_ref.at[pl.ds(0, width)]
        pl.when(is_s1)(lambda: head_copy(2, {"pcol": pcol_x}, first).start())
        pass_head(first)

    @pl.when(is_s0)
    def _():
        def send(t):
            for i in range(2):
                p, c = row_of(t, 0, i), row_of(t, 1, i)
                pl.when(far)(lambda: fwd_copy(0, p, lane_at(0, t, i), m_at(p)).start())
                remote(m_at(c), at(0, c), CROSS, lane_at(0, t, i), {"pcol": pcol_x}).start()

        loop(a0, tiles, send)

    @pl.when(is_s1)
    def _():
        def send(t):
            unit_copy(1, t, 0, own, m_ref.at[unit_of(t, 0)]).start()

        loop(a0, tiles, send)

    def split(src, dst, panel):
        rest = src[panel]
        for i in range(PIECES):
            piece = rest.astype(BF)
            dst[panel, i] = piece
            rest = rest - piece.astype(F32)

    load_u.wait()
    load_l.wait()
    split(lf, ls, 0)
    split(uf, us, 0)
    pl.when(source)(lambda: split(uf, us, 1))
    pl.when(is_g & (prow == 1))(lambda: split(lf, ls, 1))
    pl.when(is_s0)(load_lane.wait)
    pl.when(jnp.logical_not(is_s0))(load_own.wait)

    def lower_times(panel, value, out):
        upper = sum(dot(ls[panel, i, :half, :half], value[:half]) for i in reversed(range(PIECES)))
        out[:half] = upper.astype(BF)
        lower = sum(dot(ls[panel, i, half:], value) for i in reversed(range(PIECES)))
        out[half:] = lower.astype(BF)

    def take_head():
        pl.when(has_head)(load_head.wait)

        @pl.when(jnp.logical_not(has_head))
        def _():
            head_copy(0, {"prow": prow_x}).wait_recv()
            pl.when(r == 0)(pass_head)

    def make_u0():
        lower_times(0, head[...], u0)

    def out_tile(src, t):
        here = tile_of(t)
        return pltpu.make_async_copy(src.at[here], out_ref.at[here], out_sem)

    def out_first(src):
        return pltpu.make_async_copy(src, out_ref.at[pl.ds(0, width)], out_sem)

    def make_lower(t, low, lane):
        here = unit_of(t, lane)
        cur = (own[here].astype(F32) - dot(low, u0[...])).astype(BF)
        value = times_upper(cur, us, 1)
        buf[1, here] = jnp.where((prow == 1) & (t < PER), cur, value)

    def lend(t):
        @pl.when(lends & (t >= 0) & (t < moved))
        def _():
            for i in range(2):
                lend_copy(2 * t + i).start()

    def borrow():
        @pl.when(borrows)
        def _():
            def one(j):
                arrived(1, n_pkt + j, spare_at(j))
                pl.when(far)(lambda: fwd_copy(1, n_pkt + j, spare_at(j)).start())

            loop(0, 2 * moved, one)

    @pl.when(is_s0)
    def _():
        pl.when(prow == 0)(lambda: out_first(buf.at[0, pl.ds(0, width)]).start())

        def low_step(i):
            t = a0 + i
            here = tile_of(t)
            buf[0, here] = times_upper(buf[0, here], us, 0)
            out_tile(buf.at[0], t).start()
            pl.when(i == jnp.where(prow == 0, HEAD_AT, n_a - 1))(take_head)

        loop(0, n_a, low_step)
        make_u0()

        def send(t):
            for i in range(2):
                p = row_of(t, 0, i)
                pl.when(far & (t >= b0))(lambda: fwd_copy(1, p, lane_at(1, t, i)).start())
            unit_copy(1, t, 0, buf.at[1]).start()

        def step(i):
            t = a0 + i
            unit_copy(1, t, 0, own).wait_recv()
            make_lower(t, buf[0, unit_of(t, 0)], 0)
            lend(t - 1)
            pl.when(i == EARLY + 1)(borrow)
            pl.when(i >= 1)(lambda: send(t - 1))

        loop(0, n_a, step)
        send(tiles - 1)

    @pl.when(is_s1)
    def _():
        lag = 8

        def relay(t):
            for i in range(2):
                p, sem = row_of(t, 1, i), lane_at(0, t, i)
                arrived(0, p, sem)
                pl.when(far)(lambda: fwd_copy(0, p, sem).start())

        def make(t):
            make_lower(t, times_upper(buf[0, unit_of(t, 1)], us, 0), 1)
            lend(t - 1)

        def step(s):
            relay(a0 + s)
            pl.when(s == jnp.where(r == 0, PER, lag))(take_head)
            pl.when(s == lag)(make_u0)
            pl.when(s >= lag)(lambda: make(a0 + s - lag))

        loop(0, n_a, step)
        pl.when(prow == 0)(lambda: out_first(u0).start())

        def late(i):
            pl.when(i < lag)(lambda: make(tiles - lag + i))
            pl.when(i == EARLY)(borrow)
            t = b0 + i
            for n in range(2):
                pl.when(far)(lambda: fwd_copy(1, row_of(t, 1, n), lane_at(1, t, n)).start())

        loop(0, n_b, late)

        def finish(t):
            unit_copy(1, t, 0, buf.at[1]).wait_recv()
            out_tile(buf.at[1], t).start()

        loop(a0, tiles, finish)

    @pl.when(is_g)
    def _():
        lag_a = 6
        lag_b = jnp.where(x == 0, 6, 4)
        total = n_a + n_r + n_b
        cross_lent = tiles - PER + EARLY + 3
        use_lent = cross_lent + 6
        first_of_1 = lag_a + PER

        def u1_copy(i, where):
            return remote(u1, u1, hsend.at[3 + i], hrecv.at[1], where)

        def pass_u1():
            u1_copy(0, {"prow": prow - 1}).start()
            pl.when(jnp.logical_not(bottom))(lambda: u1_copy(1, {"prow": prow + 2}).start())

        def arrived_u1():
            u1_copy(0, {"prow": prow_x}).wait_recv()

        def apply_a(t):
            unit_copy(0, t, 1 - x, buf.at[0]).wait_recv()
            here = tile_of(t)
            low = times_upper(buf[0, here], us, 0)
            own[here] = (own[here].astype(F32) - dot(low, u0[...])).astype(BF)

        def apply_b(t):
            unit_copy(1, t, 1 - x, buf.at[1]).wait_recv()
            here = tile_of(t)
            own[here] = (own[here].astype(F32) - dot(buf[1, here], u1[...])).astype(BF)
            out_tile(own, t).start()

        def place(s):
            q = s - n_a
            spare = (q >= EARLY) & (q < EARLY + n_r)
            return spare, b0 + q - jnp.where(q >= EARLY + n_r, n_r, 0)

        def step(s):
            in_a = s < n_a
            spare, tb = place(s)
            in_r = jnp.logical_not(in_a) & spare
            ph = jnp.where(in_a, 0, 1)
            t = jnp.where(in_a, a0 + s, tb)

            def relay(i):
                @pl.when((s < total) & jnp.logical_not(in_r))
                def _():
                    p, sem = row_of(t, x, i), lane_at(ph, t, i)
                    arrived(ph, p, sem)
                    pl.when(far)(lambda: fwd_copy(ph, p, sem).start())
                    cross_copy(ph, t, p).start()

                @pl.when(in_r)
                def _():
                    j = 2 * (s - n_a - EARLY) + i
                    arrived(1, n_pkt + j, spare_at(j))
                    pl.when(far)(lambda: fwd_copy(1, n_pkt + j, spare_at(j)).start())
                    give_copy(j).start()

            relay(0)
            pl.when(s == jnp.where(r == 0, PER, lag_a))(take_head)
            pl.when(s == lag_a)(make_u0)
            ta = s - lag_a
            pl.when((ta >= 0) & (ta < n_a))(lambda: apply_a(a0 + ta))
            relay(1)

            @pl.when((prow == 1) & (s == first_of_1))
            def _():
                lower_times(1, own[pl.ds(0, width)], u1)

            pl.when((prow == 1) & (s == first_of_1 + 1))(pass_u1)
            pl.when((prow == 0) & (s == first_of_1 + 1))(lambda: out_first(u0).start())
            pl.when((prow == 1) & (s == first_of_1 + 1))(lambda: out_first(u1).start())

            @pl.when((r == 1) & (prow > 1) & (s == tiles - PER - 2))
            def _():
                arrived_u1()
                pass_u1()

            pl.when((r == 0) & (s == tiles - PER - 1))(arrived_u1)

            @pl.when(lends & (s >= cross_lent) & (s < cross_lent + moved))
            def _():
                k = s - cross_lent
                for i in range(2):
                    p = row_of(k, x, i)
                    arrived(1, p, lane_at(1, k, i))
                    cross_copy(1, k, p).start()

            u = s - lag_b
            u_spare, u_tile = place(u)
            n_plain = jnp.where((u >= n_a) & (u < total) & jnp.logical_not(u_spare), 1, 0)
            n_lent = jnp.where(lends & (s >= use_lent) & (s < use_lent + moved), 1, 0)
            loop(
                1 - n_plain, 1 + n_lent,
                lambda k: apply_b(jnp.where(k == 0, u_tile, s - use_lent)),
            )

        loop(0, total + lag_b, step)

        @pl.when(r == 1)
        def _():
            u1_copy(0, {"prow": prow_x}).wait_send()
            pl.when(jnp.logical_not(bottom))(lambda: u1_copy(1, {"prow": prow_x}).wait_send())

    @pl.when(r == 0)
    def _():
        head_copy(0, {"prow": prow_x}).wait_send()
        pl.when(jnp.logical_not(bottom))(lambda: head_copy(1, {"prow": prow_x}).wait_send())

    pl.when(is_s1 & (prow == 0))(lambda: head_copy(2, {"pcol": pcol_x}).wait_send())
    side = (borrows & is_g) | (lends & source)
    pl.when(side)(lambda: sent(SIDE, moved)) if moved else None
    full = 2 * tiles
    ahead = (full - 2 * PER + moved, full - PER, full - moved, full)
    pl.when(far)(lambda: sent_by_prow(FWD, ahead))
    pl.when(is_g)(lambda: sent_by_prow(CROSS, (full - 2 * PER, full - PER, full)))
    pl.when(is_s0)(lambda: sent_by_prow(CROSS, (full - 2 * PER, full)))
    pl.when(is_s1)(lambda: sent_by_prow(CROSS, (tiles - PER, tiles)))
    pltpu.make_async_copy(own, out_ref, out_sem).wait()


def body(n_prow, n_pcol, matrix, u_inverse, l_inverse):
    rows, width = matrix.shape
    tile, unit, pkt, tiles, moved = sizes(rows, width, n_prow)
    square = (width, width)
    dma = pltpu.SemaphoreType.DMA
    operands = [
        pltpu.with_memory_space_constraint(a, pltpu.HBM) for a in (matrix, u_inverse, l_inverse)
    ]
    return pl.pallas_call(
        functools.partial(kernel, n_prow, n_pcol, width),
        out_shape=jax.ShapeDtypeStruct(matrix.shape, matrix.dtype),
        in_specs=[pl.BlockSpec(memory_space=pltpu.HBM)] * 3,
        out_specs=pl.BlockSpec(memory_space=pl.ANY),
        scratch_shapes=[
            pltpu.VMEM((rows, width), BF),
            pltpu.VMEM((2, rows + moved * unit, width), BF),
            pltpu.VMEM(square, BF),
            pltpu.VMEM((2,) + square, F32),
            pltpu.VMEM((2,) + square, F32),
            pltpu.VMEM((2, PIECES) + square, BF),
            pltpu.VMEM((2, PIECES) + square, BF),
            pltpu.VMEM(square, BF),
            pltpu.VMEM(square, BF),
            dma((4,)),
            dma((4 * tiles,)),
            dma((2 * tiles,)),
            dma((3,)),
            dma((2,)),
            dma((5,)),
            dma(()),
        ],
        compiler_params=pltpu.CompilerParams(
            collective_id=0, has_side_effects=True, vmem_limit_bytes=46 * 1024 * 1024
        ),
    )(*operands)


def solution(mesh):
    run = functools.partial(body, mesh.shape["prow"], mesh.shape["pcol"])
    in_specs = (P("prow", "pcol"), P(), P())
    out_specs = P("prow", "pcol")
    return jax.shard_map(run, mesh=mesh, in_specs=in_specs, out_specs=out_specs, check_vma=False)
```

time: 105 us -> 97.2 us (0.926); the launches traced: 105 us -> 95.3 us
  Pallas kernels: 103 us -> 93.5 us
    pallas_call x1, Pallas kernels: 103 us -> 93.5 us  [body(): pl.pallas_call(functools.partial(kernel, n_prow, n_pcol, width), out_shap...]
where the time goes in v2:
time: 97.2 us; the launch traced here: 95.3 us
  Pallas kernels  93.5 us (96%)
  local copies, waits for them, and re-layouts  1.84 us (2%)
    pallas_call x1, Pallas kernels, body(): pl.pallas_call(functools.partial(kernel, n_prow, n_pcol, width), out_shap...  93.5 us

profile of v2, /device:TPU:29, one launch (start us, length us, event | category | flops | bytes accessed | tf_op | source)
XLA Modules:
  0.0 95.3 jit_solution(213587147360622759)
XLA Ops:
  0.0 93.5 %shard_map.37 = bf16[3584,512]{1,0:T(8,128)(2,1)S(1)} custom-call(bf16[3584,512]{1,0:T(8,128)(2,1)} %m_ref.1, f32[2,512,512]{2,1,0:T(8,128)} %u_hbm.1, f32[2,512,512]{2,1,0:T(8,128)} %l_hbm.1), custom_call_target="tpu_custom_call" | custom-call | tf_op jit(solution)/shard_map/pallas_call | solution.py:451
  93.5 1.8 %copy.5 = bf16[3584,512]{1,0:T(8,128)(2,1)} copy(bf16[3584,512]{1,0:T(8,128)(2,1)S(1)} %shard_map.37) | data formatting | bytes 7340032

commit v3 on v2

--- a/solution.py
+++ b/solution.py
@@ -106,13 +106,29 @@
         ref = dst.at[unit_of(t, lane)]
         return remote(ref if src is None else src, ref, CROSS, unit_at(ph, t), {"pcol": pcol_x})
 
-    def lend_copy(j):
-        return remote(at(1, row_of(j // 2, x, j % 2)), at(1, n_pkt + j), SIDE, spare_at(j), {"prow": prow - 2})
-
-    def give_copy(j):
-        return remote(
-            at(1, n_pkt + j), at(1, row_of(j // 2, x, j % 2)), SIDE, lane_at(1, j // 2, j % 2), {"prow": prow + 2}
-        )
+    def spare_row(k, i):
+        return n_pkt + row_of(k, x, i)
+
+    def spare_unit_at(k):
+        return unit_sem.at[jnp.where(k < PER, k, tiles + k - PER)]
+
+    def lend_copy(k, i):
+        return remote(at(1, row_of(k, x, i)), at(1, spare_row(k, i)), SIDE, spare_at(2 * k + i), {"prow": prow - 2})
+
+    def give_copy(k, i):
+        return remote(at(1, spare_row(k, i)), at(1, row_of(k, x, i)), SIDE, lane_at(1, k, i), {"prow": prow + 2})
+
+    def spare_cross_copy(k, i):
+        ref = at(1, spare_row(k, i))
+        return remote(ref, ref, CROSS, spare_unit_at(k), {"pcol": pcol_x})
+
+    def give_unit_copy(k):
+        src, dst = buf.at[1, unit_of(tiles + k, 1 - x)], buf.at[1, unit_of(k, 1 - x)]
+        return remote(src, dst, SIDE, unit_at(1, k), {"prow": prow + 2})
+
+    def spare_unit_arrived(k):
+        ref = buf.at[1, unit_of(tiles + k, 1 - x)]
+        remote(ref, ref, CROSS, spare_unit_at(k), {"pcol": pcol_x}).wait_recv()
 
     def sent(sem, units):
         ref = buf.at[0, pl.ds(0, units * unit)]
@@ -239,16 +255,18 @@
         @pl.when(lends & (t >= 0) & (t < moved))
         def _():
             for i in range(2):
-                lend_copy(2 * t + i).start()
+                lend_copy(t, i).start()
 
     def borrow():
         @pl.when(borrows)
         def _():
-            def one(j):
-                arrived(1, n_pkt + j, spare_at(j))
-                pl.when(far)(lambda: fwd_copy(1, n_pkt + j, spare_at(j)).start())
-
-            loop(0, 2 * moved, one)
+            def one(k):
+                for i in range(2):
+                    p, sem = spare_row(k, i), spare_at(2 * k + i)
+                    arrived(1, p, sem)
+                    pl.when(far)(lambda: fwd_copy(1, p, sem).start())
+
+            loop(0, moved, one)
 
     @pl.when(is_s0)
     def _():
@@ -324,8 +342,8 @@
         lag_a = 6
         lag_b = jnp.where(x == 0, 6, 4)
         total = n_a + n_r + n_b
-        cross_lent = tiles - PER + EARLY + 3
-        use_lent = cross_lent + 6
+        give_from = n_a + EARLY + jnp.where(x == 0, 5, 3)
+        use_lent = tiles - PER + EARLY + 9
         first_of_1 = lag_a + PER
 
         def u1_copy(i, where):
@@ -344,7 +362,12 @@
             low = times_upper(buf[0, here], us, 0)
             own[here] = (own[here].astype(F32) - dot(low, u0[...])).astype(BF)
 
-        def apply_b(t):
+        def apply_b(t, was_lent):
+            @pl.when(was_lent)
+            def _():
+                for i in range(2):
+                    arrived(1, row_of(t, x, i), lane_at(1, t, i))
+
             unit_copy(1, t, 1 - x, buf.at[1]).wait_recv()
             here = tile_of(t)
             own[here] = (own[here].astype(F32) - dot(buf[1, here], u1[...])).astype(BF)
@@ -372,10 +395,12 @@
 
                 @pl.when(in_r)
                 def _():
-                    j = 2 * (s - n_a - EARLY) + i
-                    arrived(1, n_pkt + j, spare_at(j))
-                    pl.when(far)(lambda: fwd_copy(1, n_pkt + j, spare_at(j)).start())
-                    give_copy(j).start()
+                    k = s - n_a - EARLY
+                    p, sem = spare_row(k, i), spare_at(2 * k + i)
+                    arrived(1, p, sem)
+                    pl.when(far)(lambda: fwd_copy(1, p, sem).start())
+                    spare_cross_copy(k, i).start()
+                    give_copy(k, i).start()
 
             relay(0)
             pl.when(s == jnp.where(r == 0, PER, lag_a))(take_head)
@@ -399,13 +424,10 @@
 
             pl.when((r == 0) & (s == tiles - PER - 1))(arrived_u1)
 
-            @pl.when(lends & (s >= cross_lent) & (s < cross_lent + moved))
+            @pl.when(borrows & (s >= give_from) & (s < give_from + moved))
             def _():
-                k = s - cross_lent
-                for i in range(2):
-                    p = row_of(k, x, i)
-                    arrived(1, p, lane_at(1, k, i))
-                    cross_copy(1, k, p).start()
+                spare_unit_arrived(s - give_from)
+                give_unit_copy(s - give_from).start()
 
             u = s - lag_b
             u_spare, u_tile = place(u)
@@ -413,7 +435,7 @@
             n_lent = jnp.where(lends & (s >= use_lent) & (s < use_lent + moved), 1, 0)
             loop(
                 1 - n_plain, 1 + n_lent,
-                lambda k: apply_b(jnp.where(k == 0, u_tile, s - use_lent)),
+                lambda k: apply_b(jnp.where(k == 0, u_tile, s - use_lent), k == 1),
             )
 
         loop(0, total + lag_b, step)
@@ -429,12 +451,13 @@
         pl.when(jnp.logical_not(bottom))(lambda: head_copy(1, {"prow": prow_x}).wait_send())
 
     pl.when(is_s1 & (prow == 0))(lambda: head_copy(2, {"pcol": pcol_x}).wait_send())
-    side = (borrows & is_g) | (lends & source)
-    pl.when(side)(lambda: sent(SIDE, moved)) if moved else None
+    if moved:
+        pl.when(borrows & is_g)(lambda: sent(SIDE, 2 * moved))
+        pl.when(lends & source)(lambda: sent(SIDE, moved))
     full = 2 * tiles
     ahead = (full - 2 * PER + moved, full - PER, full - moved, full)
     pl.when(far)(lambda: sent_by_prow(FWD, ahead))
-    pl.when(is_g)(lambda: sent_by_prow(CROSS, (full - 2 * PER, full - PER, full)))
+    pl.when(is_g)(lambda: sent_by_prow(CROSS, ahead))
     pl.when(is_s0)(lambda: sent_by_prow(CROSS, (full - 2 * PER, full)))
     pl.when(is_s1)(lambda: sent_by_prow(CROSS, (tiles - PER, tiles)))
     pltpu.make_async_copy(own, out_ref, out_sem).wait()
@@ -455,7 +478,7 @@
         out_specs=pl.BlockSpec(memory_space=pl.ANY),
         scratch_shapes=[
             pltpu.VMEM((rows, width), BF),
-            pltpu.VMEM((2, rows + moved * unit, width), BF),
+            pltpu.VMEM((2, rows + moved * tile, width), BF),
             pltpu.VMEM(square, BF),
             pltpu.VMEM((2,) + square, F32),
             pltpu.VMEM((2,) + square, F32),

time: 97.2 us -> 93 us (0.957); the launches traced: 95.3 us -> 92.8 us
  Pallas kernels: 93.5 us -> 91 us
    pallas_call x1, Pallas kernels: 93.5 us -> 91 us  [body(): pl.pallas_call(functools.partial(kernel, n_prow, n_pcol, width), out_shap...]
where the time goes in v3:
time: 93 us; the launch traced here: 92.8 us
  Pallas kernels  91 us (98%)
  local copies, waits for them, and re-layouts  1.84 us (2%)
    pallas_call x1, Pallas kernels, body(): pl.pallas_call(functools.partial(kernel, n_prow, n_pcol, width), out_shap...  91 us

profile of v3, /device:TPU:29, one launch (start us, length us, event | category | flops | bytes accessed | tf_op | source)
XLA Modules:
  0.0 92.8 jit_solution(321789367755042375)
XLA Ops:
  0.0 91.0 %shard_map.37 = bf16[3584,512]{1,0:T(8,128)(2,1)S(1)} custom-call(bf16[3584,512]{1,0:T(8,128)(2,1)} %m_ref.1, f32[2,512,512]{2,1,0:T(8,128)} %u_hbm.1, f32[2,512,512]{2,1,0:T(8,128)} %l_hbm.1), custom_call_target="tpu_custom_call" | custom-call | tf_op jit(solution)/shard_map/pallas_call | solution.py:474
  91.0 1.8 %copy.5 = bf16[3584,512]{1,0:T(8,128)(2,1)} copy(bf16[3584,512]{1,0:T(8,128)(2,1)S(1)} %shard_map.37) | data formatting | bytes 7340032

commit v4 on v3

--- a/solution.py
+++ b/solution.py
@@ -12,14 +12,16 @@
 F32 = jnp.float32
 PIECES = 2
 PER = 4
+SPLIT = 4
 EARLY = 8
+MID = 16
 HEAD_AT = 20
 
 
 def sizes(rows, width, n_prow):
     tile = width // PER
     moved = 3 * PER // 2 if n_prow > 2 else 0
-    return tile, tile // 2, tile // 4, rows // tile, moved
+    return tile, tile // 2, tile // 2 // SPLIT, rows // tile, moved
 
 
 def dot(a, b):
@@ -36,12 +38,12 @@
 def kernel(
     n_prow, n_pcol, width, m_ref, u_hbm, l_hbm, out_ref,
     own, buf, head, uf, lf, us, ls, u0, u1,
-    load_sem, lane_sem, unit_sem, send_sem, hrecv, hsend, out_sem,
+    load_sem, lane_sem, unit_sem, send_sem, hrecv, hsend, out_sem, credit,
 ):
     rows = own.shape[0]
     tile, unit, pkt, tiles, moved = sizes(rows, width, n_prow)
     n_pkt = rows // pkt
-    lane_pkts = 2 * tiles
+    end = tiles - 1
     half = width // 2
     prow, pcol = lax.axis_index("prow"), lax.axis_index("pcol")
     x, r = pcol % 2, prow % 2
@@ -78,17 +80,14 @@
 
     FWD, CROSS, SIDE = (send_sem.at[i] for i in range(3))
 
-    def lane_at(ph, t, i):
-        return lane_sem.at[ph * lane_pkts + 2 * t + i]
-
-    def spare_at(j):
-        return lane_sem.at[jnp.where(j < 2 * PER, j, lane_pkts + j - 2 * PER)]
-
-    def unit_at(ph, t):
-        return unit_sem.at[ph * tiles + t]
+    def lane_at(slot, i):
+        return lane_sem.at[SPLIT * slot + i]
+
+    def unit_at(slot):
+        return unit_sem.at[slot]
 
     def row_of(t, lane, i):
-        return 2 * (2 * t + lane) + i
+        return SPLIT * (2 * t + lane) + i
 
     def fwd_copy(ph, p, sem, src=None):
         ref = at(ph, p)
@@ -98,41 +97,48 @@
         ref = at(ph, p)
         remote(ref, ref, FWD, sem, {"pcol": pcol_x}).wait_recv()
 
-    def cross_copy(ph, t, p):
+    def cross_copy(ph, p, sem):
         ref = at(ph, p)
-        return remote(ref, ref, CROSS, unit_at(ph, t), {"pcol": pcol_x})
-
-    def unit_copy(ph, t, lane, dst, src=None):
+        return remote(ref, ref, CROSS, sem, {"pcol": pcol_x})
+
+    def unit_copy(t, lane, slot, dst, src=None):
         ref = dst.at[unit_of(t, lane)]
-        return remote(ref if src is None else src, ref, CROSS, unit_at(ph, t), {"pcol": pcol_x})
+        return remote(ref if src is None else src, ref, CROSS, unit_at(slot), {"pcol": pcol_x})
 
     def spare_row(k, i):
         return n_pkt + row_of(k, x, i)
 
+    def spare_at(j):
+        return lane_sem.at[jnp.where(j < SPLIT * PER, j, SPLIT * (tiles + 1 - PER) + j)]
+
     def spare_unit_at(k):
-        return unit_sem.at[jnp.where(k < PER, k, tiles + k - PER)]
+        return unit_sem.at[jnp.where(k < PER, k, tiles + 1 - PER + k)]
 
     def lend_copy(k, i):
-        return remote(at(1, row_of(k, x, i)), at(1, spare_row(k, i)), SIDE, spare_at(2 * k + i), {"prow": prow - 2})
+        return remote(at(1, row_of(k, x, i)), at(1, spare_row(k, i)), SIDE, spare_at(SPLIT * k + i), {"prow": prow - 2})
 
     def give_copy(k, i):
-        return remote(at(1, spare_row(k, i)), at(1, row_of(k, x, i)), SIDE, lane_at(1, k, i), {"prow": prow + 2})
-
-    def spare_cross_copy(k, i):
-        ref = at(1, spare_row(k, i))
-        return remote(ref, ref, CROSS, spare_unit_at(k), {"pcol": pcol_x})
+        return remote(at(1, spare_row(k, i)), at(1, row_of(k, x, i)), SIDE, lane_at(k, i), {"prow": prow + 2})
 
     def give_unit_copy(k):
         src, dst = buf.at[1, unit_of(tiles + k, 1 - x)], buf.at[1, unit_of(k, 1 - x)]
-        return remote(src, dst, SIDE, unit_at(1, k), {"prow": prow + 2})
+        return remote(src, dst, SIDE, unit_at(k), {"prow": prow + 2})
 
     def spare_unit_arrived(k):
         ref = buf.at[1, unit_of(tiles + k, 1 - x)]
         remote(ref, ref, CROSS, spare_unit_at(k), {"pcol": pcol_x}).wait_recv()
 
+    Z, X, Y = (credit.at[i] for i in range(3))
+
+    def allow(sem, where):
+        pl.semaphore_signal(sem, inc=1, device_id=where, device_id_type=MESH)
+
+    def allowed(sem):
+        pl.semaphore_wait(sem, 1)
+
     def sent(sem, units):
         ref = buf.at[0, pl.ds(0, units * unit)]
-        remote(ref, ref, sem, lane_sem.at[0], {"pcol": pcol_x}).wait_send()
+        remote(ref, ref, sem, lane_at(0, 0), {"pcol": pcol_x}).wait_send()
 
     def sent_by_prow(sem, units):
         for k, n in enumerate(units):
@@ -190,20 +196,31 @@
 
     @pl.when(is_s0)
     def _():
+        def ahead(t, lane, slot):
+            for i in range(SPLIT):
+                p = row_of(t, lane, i)
+                pl.when(far)(lambda: fwd_copy(0, p, lane_at(slot, i), m_at(p)).start())
+
+        def across(t, lane, slot):
+            for i in range(SPLIT):
+                p = row_of(t, lane, i)
+                remote(m_at(p), at(0, p), CROSS, lane_at(slot, i), {"pcol": pcol_x}).start()
+
         def send(t):
-            for i in range(2):
-                p, c = row_of(t, 0, i), row_of(t, 1, i)
-                pl.when(far)(lambda: fwd_copy(0, p, lane_at(0, t, i), m_at(p)).start())
-                remote(m_at(c), at(0, c), CROSS, lane_at(0, t, i), {"pcol": pcol_x}).start()
+            ahead(t, 0, t)
+            across(t, 1, t)
 
         loop(a0, tiles, send)
+        ahead(end, 1, tiles)
+        across(end, 0, tiles)
 
     @pl.when(is_s1)
     def _():
-        def send(t):
-            unit_copy(1, t, 0, own, m_ref.at[unit_of(t, 0)]).start()
-
-        loop(a0, tiles, send)
+        def send(t, lane, slot):
+            unit_copy(t, lane, slot, own, m_ref.at[unit_of(t, lane)]).start()
+
+        loop(a0, tiles, lambda t: send(t, 0, t))
+        send(end, 1, tiles)
 
     def split(src, dst, panel):
         rest = src[panel]
@@ -254,19 +271,25 @@
     def lend(t):
         @pl.when(lends & (t >= 0) & (t < moved))
         def _():
-            for i in range(2):
+            for i in range(SPLIT):
                 lend_copy(t, i).start()
 
     def borrow():
         @pl.when(borrows)
         def _():
             def one(k):
-                for i in range(2):
-                    p, sem = spare_row(k, i), spare_at(2 * k + i)
+                for i in range(SPLIT):
+                    p, sem = spare_row(k, i), spare_at(SPLIT * k + i)
                     arrived(1, p, sem)
                     pl.when(far)(lambda: fwd_copy(1, p, sem).start())
 
             loop(0, moved, one)
+
+    def send_lower(t, lane, slot):
+        pl.when(far & ((t == b0) | (t == MID)))(lambda: allowed(Z))
+        for i in range(SPLIT):
+            p = row_of(t, lane, i)
+            pl.when(far & (t >= b0))(lambda: fwd_copy(1, p, lane_at(slot, i)).start())
 
     @pl.when(is_s0)
     def _():
@@ -282,35 +305,38 @@
         loop(0, n_a, low_step)
         make_u0()
 
+        def make(t, lane, slot):
+            unit_copy(t, lane, slot, own).wait_recv()
+            make_lower(t, buf[0, unit_of(t, lane)], lane)
+
         def send(t):
-            for i in range(2):
-                p = row_of(t, 0, i)
-                pl.when(far & (t >= b0))(lambda: fwd_copy(1, p, lane_at(1, t, i)).start())
-            unit_copy(1, t, 0, buf.at[1]).start()
+            send_lower(t, 0, t)
+            unit_copy(t, 0, t, buf.at[1]).start()
 
         def step(i):
             t = a0 + i
-            unit_copy(1, t, 0, own).wait_recv()
-            make_lower(t, buf[0, unit_of(t, 0)], 0)
+            make(t, 0, t)
             lend(t - 1)
             pl.when(i == EARLY + 1)(borrow)
             pl.when(i >= 1)(lambda: send(t - 1))
 
         loop(0, n_a, step)
-        send(tiles - 1)
+        make(end, 1, tiles)
+        send_lower(end, 0, end)
+        send_lower(end, 1, tiles)
 
     @pl.when(is_s1)
     def _():
         lag = 8
 
         def relay(t):
-            for i in range(2):
-                p, sem = row_of(t, 1, i), lane_at(0, t, i)
+            for i in range(SPLIT):
+                p, sem = row_of(t, 1, i), lane_at(t, i)
                 arrived(0, p, sem)
                 pl.when(far)(lambda: fwd_copy(0, p, sem).start())
 
-        def make(t):
-            make_lower(t, times_upper(buf[0, unit_of(t, 1)], us, 0), 1)
+        def make(t, lane=1):
+            make_lower(t, times_upper(buf[0, unit_of(t, lane)], us, 0), lane)
             lend(t - 1)
 
         def step(s):
@@ -319,30 +345,40 @@
             pl.when(s == lag)(make_u0)
             pl.when(s >= lag)(lambda: make(a0 + s - lag))
 
-        loop(0, n_a, step)
+        loop(0, n_a - 1, step)
         pl.when(prow == 0)(lambda: out_first(u0).start())
 
         def late(i):
-            pl.when(i < lag)(lambda: make(tiles - lag + i))
             pl.when(i == EARLY)(borrow)
-            t = b0 + i
-            for n in range(2):
-                pl.when(far)(lambda: fwd_copy(1, row_of(t, 1, n), lane_at(1, t, n)).start())
+            send_lower(b0 + i, 1, b0 + i)
+
+            @pl.when(i <= lag + 1)
+            def _():
+                lane = jnp.where(i <= lag, 1, 0)
+
+                @pl.when(i >= lag)
+                def _():
+                    for n in range(SPLIT):
+                        arrived(0, row_of(end, lane, n), lane_at(tiles - lane, n))
+
+                make(jnp.minimum(end - lag + i, end), lane)
 
         loop(0, n_b, late)
+        send_lower(end, 0, tiles)
+        out_tile(buf.at[1], end).start()
 
         def finish(t):
-            unit_copy(1, t, 0, buf.at[1]).wait_recv()
+            unit_copy(t, 0, t, buf.at[1]).wait_recv()
             out_tile(buf.at[1], t).start()
 
-        loop(a0, tiles, finish)
+        loop(a0, end, finish)
 
     @pl.when(is_g)
     def _():
-        lag_a = 6
-        lag_b = jnp.where(x == 0, 6, 4)
-        total = n_a + n_r + n_b
-        give_from = n_a + EARLY + jnp.where(x == 0, 5, 3)
+        lag_a, lag_b = 6, 4
+        n_ax = n_a + 1 - 2 * x
+        total = n_ax + n_r + n_b + 1
+        give_from = n_ax + EARLY + 3
         use_lent = tiles - PER + EARLY + 9
         first_of_1 = lag_a + PER
 
@@ -357,57 +393,82 @@
             u1_copy(0, {"prow": prow_x}).wait_recv()
 
         def apply_a(t):
-            unit_copy(0, t, 1 - x, buf.at[0]).wait_recv()
+            pl.when((t < end) | (x == 1))(lambda: unit_copy(t, 1 - x, t, buf.at[0]).wait_recv())
+            pl.when((t == end) & (x == 1))(lambda: unit_copy(t, x, tiles, buf.at[0]).wait_recv())
             here = tile_of(t)
             low = times_upper(buf[0, here], us, 0)
             own[here] = (own[here].astype(F32) - dot(low, u0[...])).astype(BF)
 
         def apply_b(t, was_lent):
-            @pl.when(was_lent)
-            def _():
-                for i in range(2):
-                    arrived(1, row_of(t, x, i), lane_at(1, t, i))
-
-            unit_copy(1, t, 1 - x, buf.at[1]).wait_recv()
+            if was_lent:
+                for i in range(SPLIT):
+                    arrived(1, row_of(t, x, i), lane_at(t, i))
+
+            pl.when(t < end)(lambda: unit_copy(t, 1 - x, t, buf.at[1]).wait_recv())
             here = tile_of(t)
             own[here] = (own[here].astype(F32) - dot(buf[1, here], u1[...])).astype(BF)
             out_tile(own, t).start()
 
         def place(s):
-            q = s - n_a
-            spare = (q >= EARLY) & (q < EARLY + n_r)
-            return spare, b0 + q - jnp.where(q >= EARLY + n_r, n_r, 0)
+            q = s - n_ax
+            return (q >= EARLY) & (q < EARLY + n_r), q - jnp.where(q >= EARLY + n_r, n_r, 0)
+
+        def apply_plain(u):
+            u_spare, n = place(u)
+            plain = (u >= n_ax) & jnp.logical_not(u_spare) & (n != n_b - 1)
+            pl.when(plain)(lambda: apply_b(jnp.where(n == n_b, end, b0 + n), False))
+
+        def apply_lent(k):
+            pl.when(lends & (k >= 0) & (k < moved))(lambda: apply_b(k, True))
 
         def step(s):
-            in_a = s < n_a
-            spare, tb = place(s)
+            in_a = s < n_ax
+            spare, k = place(s)
             in_r = jnp.logical_not(in_a) & spare
+            in_b = (s >= n_ax) & (s < total) & jnp.logical_not(spare)
             ph = jnp.where(in_a, 0, 1)
-            t = jnp.where(in_a, a0 + s, tb)
-
-            def relay(i):
+            other = jnp.where(in_a, s == n_a, k == n_b)
+            t = jnp.where(other, end, jnp.where(in_a, a0 + s, b0 + k))
+            slot = jnp.where(other, tiles, t)
+            lane = jnp.where(other, 1 - x, x)
+
+            pl.when(s == jnp.where(r == 0, PER, lag_a))(take_head)
+            pl.when(s == lag_a)(make_u0)
+
+            @pl.when(in_b & ((k == 0) | (t == MID)))
+            def _():
+                allowed(X)
+                pl.when(far)(lambda: allowed(Z))
+
+            pl.when(borrows & (s == n_ax + EARLY))(lambda: allowed(Y))
+            ta = s - lag_a
+
+            def micro(i):
                 @pl.when((s < total) & jnp.logical_not(in_r))
                 def _():
-                    p, sem = row_of(t, x, i), lane_at(ph, t, i)
+                    p, sem = row_of(t, lane, i), lane_at(slot, i)
                     arrived(ph, p, sem)
                     pl.when(far)(lambda: fwd_copy(ph, p, sem).start())
-                    cross_copy(ph, t, p).start()
+                    pl.when(in_a | (t < end))(lambda: cross_copy(ph, p, unit_at(slot)).start())
 
                 @pl.when(in_r)
                 def _():
-                    k = s - n_a - EARLY
-                    p, sem = spare_row(k, i), spare_at(2 * k + i)
+                    n = s - n_ax - EARLY
+                    p, sem = spare_row(n, i), spare_at(SPLIT * n + i)
                     arrived(1, p, sem)
                     pl.when(far)(lambda: fwd_copy(1, p, sem).start())
-                    spare_cross_copy(k, i).start()
-                    give_copy(k, i).start()
-
-            relay(0)
-            pl.when(s == jnp.where(r == 0, PER, lag_a))(take_head)
-            pl.when(s == lag_a)(make_u0)
-            ta = s - lag_a
-            pl.when((ta >= 0) & (ta < n_a))(lambda: apply_a(a0 + ta))
-            relay(1)
+                    cross_copy(1, p, spare_unit_at(n)).start()
+                    give_copy(n, i).start()
+
+                pl.when((i == 1) & (ta >= 0) & (ta < n_a))(lambda: apply_a(a0 + ta))
+                pl.when(i == SPLIT - 1)(lambda: apply_plain(s - lag_b))
+                pl.when(i == 1)(lambda: apply_lent(s - use_lent))
+
+            loop(0, SPLIT, micro)
+
+            pl.when((s == MID - 1 - a0) | (s == n_ax - 1))(lambda: allow(Z, {"pcol": pcol - 2}))
+            pl.when((ta == MID - 1 - a0) | (ta == n_a - 1))(lambda: allow(X, {"pcol": pcol_x}))
+            pl.when(lends & (ta == MID - 1 - a0))(lambda: allow(Y, {"prow": prow - 2}))
 
             @pl.when((prow == 1) & (s == first_of_1))
             def _():
@@ -429,16 +490,8 @@
                 spare_unit_arrived(s - give_from)
                 give_unit_copy(s - give_from).start()
 
-            u = s - lag_b
-            u_spare, u_tile = place(u)
-            n_plain = jnp.where((u >= n_a) & (u < total) & jnp.logical_not(u_spare), 1, 0)
-            n_lent = jnp.where(lends & (s >= use_lent) & (s < use_lent + moved), 1, 0)
-            loop(
-                1 - n_plain, 1 + n_lent,
-                lambda k: apply_b(jnp.where(k == 0, u_tile, s - use_lent), k == 1),
-            )
-
-        loop(0, total + lag_b, step)
+        loop(0, total, step)
+        loop(total - lag_b, total, apply_plain)
 
         @pl.when(r == 1)
         def _():
@@ -455,11 +508,14 @@
         pl.when(borrows & is_g)(lambda: sent(SIDE, 2 * moved))
         pl.when(lends & source)(lambda: sent(SIDE, moved))
     full = 2 * tiles
-    ahead = (full - 2 * PER + moved, full - PER, full - moved, full)
-    pl.when(far)(lambda: sent_by_prow(FWD, ahead))
-    pl.when(is_g)(lambda: sent_by_prow(CROSS, ahead))
+    base = (full - 2 * PER + moved, full - PER, full - moved, full)
+    more, less = [n + 2 for n in base], [n - 2 for n in base]
+    pl.when(far & (x == 0))(lambda: sent_by_prow(FWD, more))
+    pl.when(far & (x == 1))(lambda: sent_by_prow(FWD, base))
+    pl.when(is_g & (x == 0))(lambda: sent_by_prow(CROSS, base))
+    pl.when(is_g & (x == 1))(lambda: sent_by_prow(CROSS, less))
     pl.when(is_s0)(lambda: sent_by_prow(CROSS, (full - 2 * PER, full)))
-    pl.when(is_s1)(lambda: sent_by_prow(CROSS, (tiles - PER, tiles)))
+    pl.when(is_s1)(lambda: sent_by_prow(CROSS, (tiles - PER + 1, tiles + 1)))
     pltpu.make_async_copy(own, out_ref, out_sem).wait()
 
 
@@ -478,7 +534,7 @@
         out_specs=pl.BlockSpec(memory_space=pl.ANY),
         scratch_shapes=[
             pltpu.VMEM((rows, width), BF),
-            pltpu.VMEM((2, rows + moved * tile, width), BF),
+            pltpu.VMEM((2, rows + max(moved, 1) * tile, width), BF),
             pltpu.VMEM(square, BF),
             pltpu.VMEM((2,) + square, F32),
             pltpu.VMEM((2,) + square, F32),
@@ -487,12 +543,13 @@
             pltpu.VMEM(square, BF),
             pltpu.VMEM(square, BF),
             dma((4,)),
-            dma((4 * tiles,)),
-            dma((2 * tiles,)),
+            dma((SPLIT * (tiles + 1 + max(moved - PER, 0)),)),
+            dma((tiles + 1 + max(moved - PER, 0),)),
             dma((3,)),
             dma((2,)),
             dma((5,)),
             dma(()),
+            pltpu.SemaphoreType.REGULAR((3,)),
         ],
         compiler_params=pltpu.CompilerParams(
             collective_id=0, has_side_effects=True, vmem_limit_bytes=46 * 1024 * 1024

time: 93 us -> 91.5 us (0.984)
  Pallas kernels: 91 us -> 89.3 us
    pallas_call x1, Pallas kernels: 91 us -> 89.3 us  [body(): pl.pallas_call(functools.partial(kernel, n_prow, n_pcol, width), out_shap...]
where the time goes in v4:
time: 91.5 us; the launch traced here: 91.1 us
  Pallas kernels  89.3 us (98%)
  local copies, waits for them, and re-layouts  1.84 us (2%)
    pallas_call x1, Pallas kernels, body(): pl.pallas_call(functools.partial(kernel, n_prow, n_pcol, width), out_shap...  89.3 us
    unnamed x1, local copies, waits for them, and re-layouts  1.84 us

profile of v4, /device:TPU:29, one launch (start us, length us, event | category | flops | bytes accessed | tf_op | source)
XLA Modules:
  0.0 91.1 jit_solution(8366384287033429162)
XLA Ops:
  0.0 89.3 %shard_map.37 = bf16[3584,512]{1,0:T(8,128)(2,1)S(1)} custom-call(bf16[3584,512]{1,0:T(8,128)(2,1)} %m_ref.1, f32[2,512,512]{2,1,0:T(8,128)} %u_hbm.1, f32[2,512,512]{2,1,0:T(8,128)} %l_hbm.1), custom_call_target="tpu_custom_call" | custom-call | tf_op jit(solution)/shard_map/pallas_call | solution.py:530
  89.3 1.8 %copy.5 = bf16[3584,512]{1,0:T(8,128)(2,1)} copy(bf16[3584,512]{1,0:T(8,128)(2,1)S(1)} %shard_map.37) | data formatting | bytes 7340032

commit v5 on v4

--- a/solution.py
+++ b/solution.py
@@ -16,11 +16,12 @@
 EARLY = 8
 MID = 16
 HEAD_AT = 20
+TAIL = 4
 
 
 def sizes(rows, width, n_prow):
     tile = width // PER
-    moved = 3 * PER // 2 if n_prow > 2 else 0
+    moved = (PER, PER // 2) if n_prow > 2 else (0, 0)
     return tile, tile // 2, tile // 2 // SPLIT, rows // tile, moved
 
 
@@ -36,9 +37,9 @@
 
 
 def kernel(
-    n_prow, n_pcol, width, m_ref, u_hbm, l_hbm, out_ref,
+    n_prow, n_pcol, width, m_ref, u_hbm, l_hbm, out_ref, cur_ref, low_ref, up_ref,
     own, buf, head, uf, lf, us, ls, u0, u1,
-    load_sem, lane_sem, unit_sem, send_sem, hrecv, hsend, out_sem, credit,
+    load_sem, lane_sem, unit_sem, lend_sem, send_sem, hrecv, hsend, out_sem, tail_sem, credit,
 ):
     rows = own.shape[0]
     tile, unit, pkt, tiles, moved = sizes(rows, width, n_prow)
@@ -52,12 +53,13 @@
     source, last = pcol < 2, pcol + 2 >= n_pcol
     top, bottom = prow < 2, prow + 2 >= n_prow
     far = jnp.logical_not(last)
-    lends, borrows = (prow == 2) & (moved > 0), (prow == 0) & (moved > 0)
+    mine = jnp.where(r == 0, moved[0], moved[1])
+    lends, borrows = (prow >= 2) & (prow < 4) & (mine > 0), top & (mine > 0)
 
     a0 = jnp.where(prow == 0, PER, 0)
     n_a = tiles - a0
-    n_r = jnp.where(borrows, moved, 0)
-    b0 = jnp.where(top, PER, jnp.where(lends, moved, 0))
+    n_r = jnp.where(borrows, mine, 0)
+    b0 = jnp.where(top, PER, jnp.where(lends, mine, 0))
     n_b = tiles - b0
 
     def at(ph, p):
@@ -108,14 +110,9 @@
     def spare_row(k, i):
         return n_pkt + row_of(k, x, i)
 
-    def spare_at(j):
-        return lane_sem.at[jnp.where(j < SPLIT * PER, j, SPLIT * (tiles + 1 - PER) + j)]
-
-    def spare_unit_at(k):
-        return unit_sem.at[jnp.where(k < PER, k, tiles + 1 - PER + k)]
-
-    def lend_copy(k, i):
-        return remote(at(1, row_of(k, x, i)), at(1, spare_row(k, i)), SIDE, spare_at(SPLIT * k + i), {"prow": prow - 2})
+    def lend_copy(k):
+        src, dst = buf.at[1, unit_of(k, x)], buf.at[1, unit_of(tiles + k, x)]
+        return remote(src, dst, SIDE, lend_sem.at[k], {"prow": prow - 2})
 
     def give_copy(k, i):
         return remote(at(1, spare_row(k, i)), at(1, row_of(k, x, i)), SIDE, lane_at(k, i), {"prow": prow + 2})
@@ -126,7 +123,7 @@
 
     def spare_unit_arrived(k):
         ref = buf.at[1, unit_of(tiles + k, 1 - x)]
-        remote(ref, ref, CROSS, spare_unit_at(k), {"pcol": pcol_x}).wait_recv()
+        remote(ref, ref, CROSS, unit_at(k), {"pcol": pcol_x}).wait_recv()
 
     Z, X, Y = (credit.at[i] for i in range(3))
 
@@ -269,21 +266,17 @@
         buf[1, here] = jnp.where((prow == 1) & (t < PER), cur, value)
 
     def lend(t):
-        @pl.when(lends & (t >= 0) & (t < moved))
-        def _():
-            for i in range(SPLIT):
-                lend_copy(t, i).start()
+        pl.when(lends & (t >= 0) & (t < mine))(lambda: lend_copy(t).start())
 
     def borrow():
         @pl.when(borrows)
         def _():
             def one(k):
+                lend_copy(k).wait_recv()
                 for i in range(SPLIT):
-                    p, sem = spare_row(k, i), spare_at(SPLIT * k + i)
-                    arrived(1, p, sem)
-                    pl.when(far)(lambda: fwd_copy(1, p, sem).start())
-
-            loop(0, moved, one)
+                    pl.when(far)(lambda: fwd_copy(1, spare_row(k, i), lane_at(k, i)).start())
+
+            loop(0, mine, one)
 
     def send_lower(t, lane, slot):
         pl.when(far & ((t == b0) | (t == MID)))(lambda: allowed(Z))
@@ -317,7 +310,7 @@
             t = a0 + i
             make(t, 0, t)
             lend(t - 1)
-            pl.when(i == EARLY + 1)(borrow)
+            pl.when(i == EARLY + 1 + b0 - a0)(borrow)
             pl.when(i >= 1)(lambda: send(t - 1))
 
         loop(0, n_a, step)
@@ -379,7 +372,7 @@
         n_ax = n_a + 1 - 2 * x
         total = n_ax + n_r + n_b + 1
         give_from = n_ax + EARLY + 3
-        use_lent = tiles - PER + EARLY + 9
+        use_lent = tiles - PER + EARLY + jnp.where(r == 0, 9, 14)
         first_of_1 = lag_a + PER
 
         def u1_copy(i, where):
@@ -391,6 +384,14 @@
 
         def arrived_u1():
             u1_copy(0, {"prow": prow_x}).wait_recv()
+
+        tail = tiles - TAIL
+
+        def to_tail(src, dst, t, i):
+            return pltpu.make_async_copy(src, dst.at[tile_of(t - tail)], tail_sem.at[i])
+
+        def save_u1():
+            pltpu.make_async_copy(u1, up_ref, tail_sem.at[2]).start()
 
         def apply_a(t):
             pl.when((t < end) | (x == 1))(lambda: unit_copy(t, 1 - x, t, buf.at[0]).wait_recv())
@@ -398,6 +399,7 @@
             here = tile_of(t)
             low = times_upper(buf[0, here], us, 0)
             own[here] = (own[here].astype(F32) - dot(low, u0[...])).astype(BF)
+            pl.when(t >= tail)(lambda: to_tail(own.at[here], cur_ref, t, 0).start())
 
         def apply_b(t, was_lent):
             if was_lent:
@@ -406,8 +408,13 @@
 
             pl.when(t < end)(lambda: unit_copy(t, 1 - x, t, buf.at[1]).wait_recv())
             here = tile_of(t)
-            own[here] = (own[here].astype(F32) - dot(buf[1, here], u1[...])).astype(BF)
-            out_tile(own, t).start()
+
+            @pl.when(t < tail)
+            def _():
+                own[here] = (own[here].astype(F32) - dot(buf[1, here], u1[...])).astype(BF)
+                out_tile(own, t).start()
+
+            pl.when(t >= tail)(lambda: to_tail(buf.at[1, here], low_ref, t, 1).start())
 
         def place(s):
             q = s - n_ax
@@ -419,7 +426,7 @@
             pl.when(plain)(lambda: apply_b(jnp.where(n == n_b, end, b0 + n), False))
 
         def apply_lent(k):
-            pl.when(lends & (k >= 0) & (k < moved))(lambda: apply_b(k, True))
+            pl.when(lends & (k >= 0) & (k < mine))(lambda: apply_b(k, True))
 
         def step(s):
             in_a = s < n_ax
@@ -454,10 +461,10 @@
                 @pl.when(in_r)
                 def _():
                     n = s - n_ax - EARLY
-                    p, sem = spare_row(n, i), spare_at(SPLIT * n + i)
+                    p, sem = spare_row(n, i), lane_at(n, i)
                     arrived(1, p, sem)
                     pl.when(far)(lambda: fwd_copy(1, p, sem).start())
-                    cross_copy(1, p, spare_unit_at(n)).start()
+                    cross_copy(1, p, unit_at(n)).start()
                     give_copy(n, i).start()
 
                 pl.when((i == 1) & (ta >= 0) & (ta < n_a))(lambda: apply_a(a0 + ta))
@@ -475,6 +482,7 @@
                 lower_times(1, own[pl.ds(0, width)], u1)
 
             pl.when((prow == 1) & (s == first_of_1 + 1))(pass_u1)
+            pl.when(s == tiles - PER)(save_u1)
             pl.when((prow == 0) & (s == first_of_1 + 1))(lambda: out_first(u0).start())
             pl.when((prow == 1) & (s == first_of_1 + 1))(lambda: out_first(u1).start())
 
@@ -485,13 +493,18 @@
 
             pl.when((r == 0) & (s == tiles - PER - 1))(arrived_u1)
 
-            @pl.when(borrows & (s >= give_from) & (s < give_from + moved))
+            @pl.when(borrows & (s >= give_from) & (s < give_from + mine))
             def _():
                 spare_unit_arrived(s - give_from)
                 give_unit_copy(s - give_from).start()
 
         loop(0, total, step)
         loop(total - lag_b, total, apply_plain)
+
+        for i, (src, dst) in enumerate(((own, cur_ref), (own, low_ref), (u1, up_ref))):
+            pltpu.make_async_copy(src.at[pl.ds(0, dst.shape[0])], dst, tail_sem.at[i]).wait()
+        done = pl.ds(0, tail * tile)
+        pltpu.make_async_copy(own.at[done], out_ref.at[done], out_sem).wait()
 
         @pl.when(r == 1)
         def _():
@@ -504,11 +517,12 @@
         pl.when(jnp.logical_not(bottom))(lambda: head_copy(1, {"prow": prow_x}).wait_send())
 
     pl.when(is_s1 & (prow == 0))(lambda: head_copy(2, {"pcol": pcol_x}).wait_send())
-    if moved:
-        pl.when(borrows & is_g)(lambda: sent(SIDE, 2 * moved))
-        pl.when(lends & source)(lambda: sent(SIDE, moved))
+    for k, n in enumerate(moved):
+        if n:
+            pl.when(is_g & (prow == k))(functools.partial(sent, SIDE, 2 * n))
+            pl.when(source & (prow == k + 2))(functools.partial(sent, SIDE, n))
     full = 2 * tiles
-    base = (full - 2 * PER + moved, full - PER, full - moved, full)
+    base = [full - 2 * PER + moved[0], full - PER + moved[1], full - moved[0], full - moved[1], full]
     more, less = [n + 2 for n in base], [n - 2 for n in base]
     pl.when(far & (x == 0))(lambda: sent_by_prow(FWD, more))
     pl.when(far & (x == 1))(lambda: sent_by_prow(FWD, base))
@@ -516,7 +530,27 @@
     pl.when(is_g & (x == 1))(lambda: sent_by_prow(CROSS, less))
     pl.when(is_s0)(lambda: sent_by_prow(CROSS, (full - 2 * PER, full)))
     pl.when(is_s1)(lambda: sent_by_prow(CROSS, (tiles - PER + 1, tiles + 1)))
-    pltpu.make_async_copy(own, out_ref, out_sem).wait()
+    pl.when(source)(lambda: pltpu.make_async_copy(own, out_ref, out_sem).wait())
+
+
+def finish(main_ref, cur_ref, low_ref, up_ref, out_ref, res, sem):
+    pcol = lax.axis_index("pcol")
+    rows, late = main_ref.shape[0], cur_ref.shape[0]
+    done = pl.ds(0, rows - late)
+    rest = pl.ds(rows - late, late)
+    bulk = pltpu.make_async_copy(main_ref.at[done], out_ref.at[done], sem.at[0])
+    bulk.start()
+    through = pltpu.make_async_copy(main_ref.at[rest], out_ref.at[rest], sem.at[1])
+    made = pltpu.make_async_copy(res, out_ref.at[rest], sem.at[1])
+    pl.when(pcol < 2)(through.start)
+
+    @pl.when(pcol >= 2)
+    def _():
+        res[...] = (cur_ref[...].astype(F32) - dot(low_ref[...], up_ref[...])).astype(BF)
+        made.start()
+
+    bulk.wait()
+    made.wait()
 
 
 def body(n_prow, n_pcol, matrix, u_inverse, l_inverse):
@@ -527,14 +561,15 @@
     operands = [
         pltpu.with_memory_space_constraint(a, pltpu.HBM) for a in (matrix, u_inverse, l_inverse)
     ]
-    return pl.pallas_call(
+    tail = (TAIL * tile, width)
+    pieces = pl.pallas_call(
         functools.partial(kernel, n_prow, n_pcol, width),
-        out_shape=jax.ShapeDtypeStruct(matrix.shape, matrix.dtype),
+        out_shape=[jax.ShapeDtypeStruct(shape, BF) for shape in (matrix.shape, tail, tail, square)],
         in_specs=[pl.BlockSpec(memory_space=pltpu.HBM)] * 3,
-        out_specs=pl.BlockSpec(memory_space=pl.ANY),
+        out_specs=[pl.BlockSpec(memory_space=pl.ANY)] * 4,
         scratch_shapes=[
             pltpu.VMEM((rows, width), BF),
-            pltpu.VMEM((2, rows + max(moved, 1) * tile, width), BF),
+            pltpu.VMEM((2, rows + PER * tile, width), BF),
             pltpu.VMEM(square, BF),
             pltpu.VMEM((2,) + square, F32),
             pltpu.VMEM((2,) + square, F32),
@@ -543,18 +578,28 @@
             pltpu.VMEM(square, BF),
             pltpu.VMEM(square, BF),
             dma((4,)),
-            dma((SPLIT * (tiles + 1 + max(moved - PER, 0)),)),
-            dma((tiles + 1 + max(moved - PER, 0),)),
+            dma((SPLIT * (tiles + 1),)),
+            dma((tiles + 1,)),
+            dma((PER,)),
             dma((3,)),
             dma((2,)),
             dma((5,)),
             dma(()),
+            dma((3,)),
             pltpu.SemaphoreType.REGULAR((3,)),
         ],
         compiler_params=pltpu.CompilerParams(
             collective_id=0, has_side_effects=True, vmem_limit_bytes=46 * 1024 * 1024
         ),
     )(*operands)
+    return pl.pallas_call(
+        finish,
+        out_shape=jax.ShapeDtypeStruct(matrix.shape, BF),
+        in_specs=[pl.BlockSpec(memory_space=pl.ANY)] + [pl.BlockSpec(memory_space=pltpu.VMEM)] * 3,
+        out_specs=pl.BlockSpec(memory_space=pl.ANY),
+        scratch_shapes=[pltpu.VMEM(tail, BF), dma((2,))],
+        compiler_params=pltpu.CompilerParams(vmem_limit_bytes=8 * 1024 * 1024),
+    )(*pieces)
 
 
 def solution(mesh):

time: 91.5 us -> 89.8 us (0.981)
  local copies, waits for them, and re-layouts: 1.84 us -> 0 us
    pallas_call x0 -> x1, Pallas kernels: none -> 1.85 us  [body(): pl.pallas_call(finish, out_shape=jax.ShapeDtypeStruct(matrix.shape, BF),...]
    unnamed x1 -> x0, local copies, waits for them, and re-layouts: 1.84 us -> none
    pallas_call x1, Pallas kernels: 89.3 us -> 87.8 us  [body(): pl.pallas_call(functools.partial(kernel, n_prow, n_pcol, width), out_shap...]
where the time goes in v5:
time: 89.8 us; the launch traced here: 89.6 us
  Pallas kernels  89.6 us (100%)
    pallas_call x1, Pallas kernels, body(): pl.pallas_call(functools.partial(kernel, n_prow, n_pcol, width), out_shap...  87.8 us
    pallas_call x1, Pallas kernels, body(): pl.pallas_call(finish, out_shape=jax.ShapeDtypeStruct(matrix.shape, BF),...  1.85 us

profile of v5, /device:TPU:29, one launch (start us, length us, event | category | flops | bytes accessed | tf_op | source)
XLA Modules:
  0.0 89.6 jit_solution(3816165319077062607)
XLA Ops:
  0.0 87.8 %shard_map.37 = (bf16[3584,512]{1,0:T(8,128)(2,1)S(1)}, bf16[512,512]{1,0:T(8,128)(2,1)S(1)}, bf16[512,512]{1,0:T(8,128)(2,1)S(1)}, bf16[512,512]{1,0:T(8,128)(2,1)S(1)}) custom-call(bf16[3584,512]{1,0:T(8,128)(2,1)} %m_ref.1, f32[2,512,512]{2,1,0:T(8,128)} %u_hbm.1, f32[2,512,512]{2,1,0:T(8,128)} %l_hbm.1), custom_call_target="tpu_custom_call" | custom-call | tf_op jit(solution)/shard_map/pallas_call | solution.py:565
  87.8 1.8 %shard_map.38 = bf16[3584,512]{1,0:T(8,128)(2,1)} custom-call(bf16[3584,512]{1,0:T(8,128)(2,1)S(1)} %get-tuple-element.9.main_ref, bf16[512,512]{1,0:T(8,128)(2,1)S(1)} %get-tuple-element.10.cur_ref, bf16[512,512]{1,0:T(8,128)(2,1)S(1)} %get-tuple-element.11.low_ref, bf16[512,512]{1,0:T(8,128)(2,1)S(1)} %get-tuple-element.12.up_ref), custom_call_target="tpu_custom_call" | custom-call | tf_op jit(solution)/shard_map/pallas_call | solution.py:595

commit v6 on v5

--- a/solution.py
+++ b/solution.py
@@ -37,9 +37,9 @@
 
 
 def kernel(
-    n_prow, n_pcol, width, m_ref, u_hbm, l_hbm, out_ref, cur_ref, low_ref, up_ref,
-    own, buf, head, uf, lf, us, ls, u0, u1,
-    load_sem, lane_sem, unit_sem, lend_sem, send_sem, hrecv, hsend, out_sem, tail_sem, credit,
+    n_prow, n_pcol, width, m_ref, u_hbm, l_hbm, own, buf, u1,
+    head, uf, lf, us, ls, u0,
+    load_sem, lane_sem, unit_sem, lend_sem, send_sem, hrecv, hsend, credit,
 ):
     rows = own.shape[0]
     tile, unit, pkt, tiles, moved = sizes(rows, width, n_prow)
@@ -252,13 +252,6 @@
     def make_u0():
         lower_times(0, head[...], u0)
 
-    def out_tile(src, t):
-        here = tile_of(t)
-        return pltpu.make_async_copy(src.at[here], out_ref.at[here], out_sem)
-
-    def out_first(src):
-        return pltpu.make_async_copy(src, out_ref.at[pl.ds(0, width)], out_sem)
-
     def make_lower(t, low, lane):
         here = unit_of(t, lane)
         cur = (own[here].astype(F32) - dot(low, u0[...])).astype(BF)
@@ -286,13 +279,10 @@
 
     @pl.when(is_s0)
     def _():
-        pl.when(prow == 0)(lambda: out_first(buf.at[0, pl.ds(0, width)]).start())
-
         def low_step(i):
             t = a0 + i
             here = tile_of(t)
             buf[0, here] = times_upper(buf[0, here], us, 0)
-            out_tile(buf.at[0], t).start()
             pl.when(i == jnp.where(prow == 0, HEAD_AT, n_a - 1))(take_head)
 
         loop(0, n_a, low_step)
@@ -339,7 +329,10 @@
             pl.when(s >= lag)(lambda: make(a0 + s - lag))
 
         loop(0, n_a - 1, step)
-        pl.when(prow == 0)(lambda: out_first(u0).start())
+
+        @pl.when(prow == 0)
+        def _():
+            buf[1, :width] = u0[...]
 
         def late(i):
             pl.when(i == EARLY)(borrow)
@@ -358,11 +351,9 @@
 
         loop(0, n_b, late)
         send_lower(end, 0, tiles)
-        out_tile(buf.at[1], end).start()
 
         def finish(t):
             unit_copy(t, 0, t, buf.at[1]).wait_recv()
-            out_tile(buf.at[1], t).start()
 
         loop(a0, end, finish)
 
@@ -387,19 +378,12 @@
 
         tail = tiles - TAIL
 
-        def to_tail(src, dst, t, i):
-            return pltpu.make_async_copy(src, dst.at[tile_of(t - tail)], tail_sem.at[i])
-
-        def save_u1():
-            pltpu.make_async_copy(u1, up_ref, tail_sem.at[2]).start()
-
         def apply_a(t):
             pl.when((t < end) | (x == 1))(lambda: unit_copy(t, 1 - x, t, buf.at[0]).wait_recv())
             pl.when((t == end) & (x == 1))(lambda: unit_copy(t, x, tiles, buf.at[0]).wait_recv())
             here = tile_of(t)
             low = times_upper(buf[0, here], us, 0)
             own[here] = (own[here].astype(F32) - dot(low, u0[...])).astype(BF)
-            pl.when(t >= tail)(lambda: to_tail(own.at[here], cur_ref, t, 0).start())
 
         def apply_b(t, was_lent):
             if was_lent:
@@ -412,9 +396,6 @@
             @pl.when(t < tail)
             def _():
                 own[here] = (own[here].astype(F32) - dot(buf[1, here], u1[...])).astype(BF)
-                out_tile(own, t).start()
-
-            pl.when(t >= tail)(lambda: to_tail(buf.at[1, here], low_ref, t, 1).start())
 
         def place(s):
             q = s - n_ax
@@ -482,9 +463,13 @@
                 lower_times(1, own[pl.ds(0, width)], u1)
 
             pl.when((prow == 1) & (s == first_of_1 + 1))(pass_u1)
-            pl.when(s == tiles - PER)(save_u1)
-            pl.when((prow == 0) & (s == first_of_1 + 1))(lambda: out_first(u0).start())
-            pl.when((prow == 1) & (s == first_of_1 + 1))(lambda: out_first(u1).start())
+            @pl.when((prow == 0) & (s == first_of_1))
+            def _():
+                own[:width] = u0[...]
+
+            @pl.when((prow == 1) & (s == first_of_1 + 1))
+            def _():
+                own[:width] = u1[...]
 
             @pl.when((r == 1) & (prow > 1) & (s == tiles - PER - 2))
             def _():
@@ -500,11 +485,6 @@
 
         loop(0, total, step)
         loop(total - lag_b, total, apply_plain)
-
-        for i, (src, dst) in enumerate(((own, cur_ref), (own, low_ref), (u1, up_ref))):
-            pltpu.make_async_copy(src.at[pl.ds(0, dst.shape[0])], dst, tail_sem.at[i]).wait()
-        done = pl.ds(0, tail * tile)
-        pltpu.make_async_copy(own.at[done], out_ref.at[done], out_sem).wait()
 
         @pl.when(r == 1)
         def _():
@@ -530,27 +510,26 @@
     pl.when(is_g & (x == 1))(lambda: sent_by_prow(CROSS, less))
     pl.when(is_s0)(lambda: sent_by_prow(CROSS, (full - 2 * PER, full)))
     pl.when(is_s1)(lambda: sent_by_prow(CROSS, (tiles - PER + 1, tiles + 1)))
-    pl.when(source)(lambda: pltpu.make_async_copy(own, out_ref, out_sem).wait())
-
-
-def finish(main_ref, cur_ref, low_ref, up_ref, out_ref, res, sem):
+
+
+def finish(own, buf, u1, out_ref, res, sem):
     pcol = lax.axis_index("pcol")
-    rows, late = main_ref.shape[0], cur_ref.shape[0]
-    done = pl.ds(0, rows - late)
-    rest = pl.ds(rows - late, late)
-    bulk = pltpu.make_async_copy(main_ref.at[done], out_ref.at[done], sem.at[0])
-    bulk.start()
-    through = pltpu.make_async_copy(main_ref.at[rest], out_ref.at[rest], sem.at[1])
-    made = pltpu.make_async_copy(res, out_ref.at[rest], sem.at[1])
-    pl.when(pcol < 2)(through.start)
+    rows, late = own.shape[0], res.shape[0]
+    whole, done, rest = pl.ds(0, rows), pl.ds(0, rows - late), pl.ds(rows - late, late)
+    for i in range(2):
+        copy = pltpu.make_async_copy(buf.at[i, whole], out_ref, sem.at[0])
+        pl.when(pcol == i)(copy.start)
+        pl.when(pcol == i)(copy.wait)
 
     @pl.when(pcol >= 2)
     def _():
-        res[...] = (cur_ref[...].astype(F32) - dot(low_ref[...], up_ref[...])).astype(BF)
+        bulk = pltpu.make_async_copy(own.at[done], out_ref.at[done], sem.at[0])
+        made = pltpu.make_async_copy(res, out_ref.at[rest], sem.at[1])
+        bulk.start()
+        res[...] = (own[rest].astype(F32) - dot(buf[1, rest], u1[...])).astype(BF)
         made.start()
-
-    bulk.wait()
-    made.wait()
+        bulk.wait()
+        made.wait()
 
 
 def body(n_prow, n_pcol, matrix, u_inverse, l_inverse):
@@ -561,21 +540,18 @@
     operands = [
         pltpu.with_memory_space_constraint(a, pltpu.HBM) for a in (matrix, u_inverse, l_inverse)
     ]
-    tail = (TAIL * tile, width)
+    lanes = (2, rows + PER * tile, width)
     pieces = pl.pallas_call(
         functools.partial(kernel, n_prow, n_pcol, width),
-        out_shape=[jax.ShapeDtypeStruct(shape, BF) for shape in (matrix.shape, tail, tail, square)],
+        out_shape=[jax.ShapeDtypeStruct(shape, BF) for shape in (matrix.shape, lanes, square)],
         in_specs=[pl.BlockSpec(memory_space=pltpu.HBM)] * 3,
-        out_specs=[pl.BlockSpec(memory_space=pl.ANY)] * 4,
+        out_specs=[pl.BlockSpec(memory_space=pltpu.VMEM)] * 3,
         scratch_shapes=[
-            pltpu.VMEM((rows, width), BF),
-            pltpu.VMEM((2, rows + PER * tile, width), BF),
             pltpu.VMEM(square, BF),
             pltpu.VMEM((2,) + square, F32),
             pltpu.VMEM((2,) + square, F32),
             pltpu.VMEM((2, PIECES) + square, BF),
             pltpu.VMEM((2, PIECES) + square, BF),
-            pltpu.VMEM(square, BF),
             pltpu.VMEM(square, BF),
             dma((4,)),
             dma((SPLIT * (tiles + 1),)),
@@ -584,20 +560,18 @@
             dma((3,)),
             dma((2,)),
             dma((5,)),
-            dma(()),
-            dma((3,)),
             pltpu.SemaphoreType.REGULAR((3,)),
         ],
         compiler_params=pltpu.CompilerParams(
-            collective_id=0, has_side_effects=True, vmem_limit_bytes=46 * 1024 * 1024
+            collective_id=0, has_side_effects=True, vmem_limit_bytes=40 * 1024 * 1024
         ),
     )(*operands)
     return pl.pallas_call(
         finish,
         out_shape=jax.ShapeDtypeStruct(matrix.shape, BF),
-        in_specs=[pl.BlockSpec(memory_space=pl.ANY)] + [pl.BlockSpec(memory_space=pltpu.VMEM)] * 3,
+        in_specs=[pl.BlockSpec(memory_space=pltpu.VMEM)] * 3,
         out_specs=pl.BlockSpec(memory_space=pl.ANY),
-        scratch_shapes=[pltpu.VMEM(tail, BF), dma((2,))],
+        scratch_shapes=[pltpu.VMEM((TAIL * tile, width), BF), dma((2,))],
         compiler_params=pltpu.CompilerParams(vmem_limit_bytes=8 * 1024 * 1024),
     )(*pieces)
 

time: 89.8 us -> 89 us (level)
  Pallas kernels: 89.6 us -> 88.5 us
    pallas_call x1, Pallas kernels: 87.8 us -> 86.6 us  [body(): pl.pallas_call(functools.partial(kernel, n_prow, n_pcol, width), out_shap...]
where the time goes in v6:
time: 89 us; the launch traced here: 88.5 us
  Pallas kernels  88.5 us (99%)
    pallas_call x1, Pallas kernels, body(): pl.pallas_call(functools.partial(kernel, n_prow, n_pcol, width), out_shap...  86.6 us
    pallas_call x1, Pallas kernels, body(): pl.pallas_call(finish, out_shape=jax.ShapeDtypeStruct(matrix.shape, BF),...  1.87 us

profile of v6, /device:TPU:29, one launch (start us, length us, event | category | flops | bytes accessed | tf_op | source)
XLA Modules:
  0.0 88.5 jit_solution(7470154180645575238)
XLA Ops:
  0.0 86.6 %shard_map.37 = (bf16[3584,512]{1,0:T(8,128)(2,1)S(1)}, bf16[2,4096,512]{2,1,0:T(8,128)(2,1)S(1)}, bf16[512,512]{1,0:T(8,128)(2,1)S(1)}) custom-call(bf16[3584,512]{1,0:T(8,128)(2,1)} %m_ref.1, f32[2,512,512]{2,1,0:T(8,128)} %u_hbm.1, f32[2,512,512]{2,1,0:T(8,128)} %l_hbm.1), custom_call_target="tpu_custom_call" | custom-call | tf_op jit(solution)/shard_map/pallas_call | solution.py:544
  86.6 1.9 %shard_map.38 = bf16[3584,512]{1,0:T(8,128)(2,1)} custom-call(bf16[3584,512]{1,0:T(8,128)(2,1)S(1)} %get-tuple-element.8.own, bf16[2,4096,512]{2,1,0:T(8,128)(2,1)S(1)} %get-tuple-element.9.buf, bf16[512,512]{1,0:T(8,128)(2,1)S(1)} %get-tuple-element.10.u1), custom_call_target="tpu_custom_call" | custom-call | tf_op jit(solution)/shard_map/pallas_call | solution.py:569

commit v7 on v6

--- a/solution.py
+++ b/solution.py
@@ -38,7 +38,7 @@
 
 def kernel(
     n_prow, n_pcol, width, m_ref, u_hbm, l_hbm, own, buf, u1,
-    head, uf, lf, us, ls, u0,
+    low_now, head, uf, lf, us, ls, u0,
     load_sem, lane_sem, unit_sem, lend_sem, send_sem, hrecv, hsend, credit,
 ):
     rows = own.shape[0]
@@ -155,11 +155,6 @@
     load_l = pltpu.make_async_copy(l_hbm, lf, load_sem.at[2])
     has_head = (prow == 0) & (pcol >= 1)
     load_head = pltpu.make_async_copy(m_ref.at[pl.ds(0, width)], head, load_sem.at[3])
-    pl.when(has_head)(load_head.start)
-    load_u.start()
-    load_l.start()
-    pl.when(is_s0)(load_lane.start)
-    pl.when(jnp.logical_not(is_s0))(load_own.start)
 
     barrier = pltpu.get_barrier_semaphore()
 
@@ -175,6 +170,11 @@
         (jnp.logical_not(bottom), {"prow": prow + 2}),
     ):
         pl.when(ok)(functools.partial(greet, where))
+    pl.when(has_head)(load_head.start)
+    load_u.start()
+    load_l.start()
+    pl.when(is_s0)(load_lane.start)
+    pl.when(jnp.logical_not(is_s0))(load_own.start)
     absent = [jnp.where(ok, 1, 0) for ok in (source, last, top, bottom)]
     pl.semaphore_wait(barrier, 6 - sum(absent))
 
@@ -312,21 +312,33 @@
     def _():
         lag = 8
 
-        def relay(t):
-            for i in range(SPLIT):
-                p, sem = row_of(t, 1, i), lane_at(t, i)
-                arrived(0, p, sem)
-                pl.when(far)(lambda: fwd_copy(0, p, sem).start())
+        def relay(t, i):
+            p, sem = row_of(t, 1, i), lane_at(t, i)
+            arrived(0, p, sem)
+            pl.when(far)(lambda: fwd_copy(0, p, sem).start())
+
+        def make_part(t, i):
+            here, low, cur = unit_of(t, 1), slice(0, unit), slice(unit, tile)
+            if i == 0:
+                low_now[low] = times_upper(buf[0, here], us, 0)
+            elif i == 1:
+                low_now[cur] = (own[here].astype(F32) - dot(low_now[low], u0[...])).astype(BF)
+            elif i == 2:
+                value = times_upper(low_now[cur], us, 1)
+                buf[1, here] = jnp.where((prow == 1) & (t < PER), low_now[cur], value)
+            else:
+                lend(t - 1)
 
         def make(t, lane=1):
             make_lower(t, times_upper(buf[0, unit_of(t, lane)], us, 0), lane)
             lend(t - 1)
 
         def step(s):
-            relay(a0 + s)
             pl.when(s == jnp.where(r == 0, PER, lag))(take_head)
             pl.when(s == lag)(make_u0)
-            pl.when(s >= lag)(lambda: make(a0 + s - lag))
+            for i in range(SPLIT):
+                relay(a0 + s, i)
+                pl.when(s >= lag)(functools.partial(make_part, a0 + s - lag, i))
 
         loop(0, n_a - 1, step)
 
@@ -378,12 +390,14 @@
 
         tail = tiles - TAIL
 
-        def apply_a(t):
+        def lower_a(t):
             pl.when((t < end) | (x == 1))(lambda: unit_copy(t, 1 - x, t, buf.at[0]).wait_recv())
             pl.when((t == end) & (x == 1))(lambda: unit_copy(t, x, tiles, buf.at[0]).wait_recv())
+            low_now[...] = times_upper(buf[0, tile_of(t)], us, 0)
+
+        def apply_a(t):
             here = tile_of(t)
-            low = times_upper(buf[0, here], us, 0)
-            own[here] = (own[here].astype(F32) - dot(low, u0[...])).astype(BF)
+            own[here] = (own[here].astype(F32) - dot(low_now[...], u0[...])).astype(BF)
 
         def apply_b(t, was_lent):
             if was_lent:
@@ -448,6 +462,7 @@
                     cross_copy(1, p, unit_at(n)).start()
                     give_copy(n, i).start()
 
+                pl.when((i == 0) & (ta >= 0) & (ta < n_a))(lambda: lower_a(a0 + ta))
                 pl.when((i == 1) & (ta >= 0) & (ta < n_a))(lambda: apply_a(a0 + ta))
                 pl.when(i == SPLIT - 1)(lambda: apply_plain(s - lag_b))
                 pl.when(i == 1)(lambda: apply_lent(s - use_lent))
@@ -547,6 +562,7 @@
         in_specs=[pl.BlockSpec(memory_space=pltpu.HBM)] * 3,
         out_specs=[pl.BlockSpec(memory_space=pltpu.VMEM)] * 3,
         scratch_shapes=[
+            pltpu.VMEM((tile, width), BF),
             pltpu.VMEM(square, BF),
             pltpu.VMEM((2,) + square, F32),
             pltpu.VMEM((2,) + square, F32),

time: 89 us -> 88.7 us (level)
  no operation moved by 1% of the time
where the time goes in v7:
time: 88.7 us; the launch traced here: 88.5 us
  Pallas kernels  88.5 us (100%)
    pallas_call x1, Pallas kernels, body(): pl.pallas_call(functools.partial(kernel, n_prow, n_pcol, width), out_shap...  86.6 us
    pallas_call x1, Pallas kernels, body(): pl.pallas_call(finish, out_shape=jax.ShapeDtypeStruct(matrix.shape, BF),...  1.87 us

profile of v7, /device:TPU:29, one launch (start us, length us, event | category | flops | bytes accessed | tf_op | source)
XLA Modules:
  0.0 88.5 jit_solution(9605666215696513765)
XLA Ops:
  0.0 86.6 %shard_map.37 = (bf16[3584,512]{1,0:T(8,128)(2,1)S(1)}, bf16[2,4096,512]{2,1,0:T(8,128)(2,1)S(1)}, bf16[512,512]{1,0:T(8,128)(2,1)S(1)}) custom-call(bf16[3584,512]{1,0:T(8,128)(2,1)} %m_ref.1, f32[2,512,512]{2,1,0:T(8,128)} %u_hbm.1, f32[2,512,512]{2,1,0:T(8,128)} %l_hbm.1), custom_call_target="tpu_custom_call" | custom-call | tf_op jit(solution)/shard_map/pallas_call | solution.py:559
  86.7 1.9 %shard_map.38 = bf16[3584,512]{1,0:T(8,128)(2,1)} custom-call(bf16[3584,512]{1,0:T(8,128)(2,1)S(1)} %get-tuple-element.8.own, bf16[2,4096,512]{2,1,0:T(8,128)(2,1)S(1)} %get-tuple-element.9.buf, bf16[512,512]{1,0:T(8,128)(2,1)S(1)} %get-tuple-element.10.u1), custom_call_target="tpu_custom_call" | custom-call | tf_op jit(solution)/shard_map/pallas_call | solution.py:585

commit v8 on v7

--- a/solution.py
+++ b/solution.py
@@ -15,6 +15,7 @@
 SPLIT = 4
 EARLY = 8
 MID = 16
+RING, BLOCK = 14, 7
 HEAD_AT = 20
 TAIL = 4
 
@@ -61,6 +62,8 @@
     n_r = jnp.where(borrows, mine, 0)
     b0 = jnp.where(top, PER, jnp.where(lends, mine, 0))
     n_b = tiles - b0
+    n_ax = n_a + 1 - 2 * x
+    total = n_ax + n_r + n_b + 1
 
     def at(ph, p):
         return buf.at[ph, pl.ds(pl.multiple_of(p * pkt, pkt), pkt)]
@@ -82,8 +85,8 @@
 
     FWD, CROSS, SIDE = (send_sem.at[i] for i in range(3))
 
-    def lane_at(slot, i):
-        return lane_sem.at[SPLIT * slot + i]
+    def lane_at(s, i):
+        return lane_sem.at[SPLIT * (s % RING) + i]
 
     def unit_at(slot):
         return unit_sem.at[slot]
@@ -114,8 +117,9 @@
         src, dst = buf.at[1, unit_of(k, x)], buf.at[1, unit_of(tiles + k, x)]
         return remote(src, dst, SIDE, lend_sem.at[k], {"prow": prow - 2})
 
-    def give_copy(k, i):
-        return remote(at(1, spare_row(k, i)), at(1, row_of(k, x, i)), SIDE, lane_at(k, i), {"prow": prow + 2})
+    def give_copy(k):
+        src, dst = buf.at[1, unit_of(tiles + k, x)], buf.at[1, unit_of(k, x)]
+        return remote(src, dst, SIDE, lend_sem.at[k], {"prow": prow + 2})
 
     def give_unit_copy(k):
         src, dst = buf.at[1, unit_of(tiles + k, 1 - x)], buf.at[1, unit_of(k, 1 - x)]
@@ -132,6 +136,15 @@
 
     def allowed(sem):
         pl.semaphore_wait(sem, 1)
+
+    def gate(s, sem=Z):
+        pl.when((s >= RING) & (s % BLOCK == 0))(lambda: allowed(sem))
+
+    def open_gate(s, steps, sem, where):
+        pl.when((s % BLOCK == BLOCK - 1) & (s + BLOCK + 1 < steps))(lambda: allow(sem, where))
+
+    def step_of(k):
+        return n_ax + k + jnp.where(k >= EARLY, n_r, 0)
 
     def sent(sem, units):
         ref = buf.at[0, pl.ds(0, units * unit)]
@@ -191,25 +204,18 @@
         pl.when(is_s1)(lambda: head_copy(2, {"pcol": pcol_x}, first).start())
         pass_head(first)
 
+    def push(s):
+        pl.when(far)(lambda: gate(s))
+        gate(s, X)
+        t, lane = jnp.where(s < n_a, a0 + s, end), jnp.where(s < n_a, 0, 1)
+        for i in range(SPLIT):
+            p, c = row_of(t, lane, i), row_of(t, 1 - lane, i)
+            pl.when(far)(lambda: fwd_copy(0, p, lane_at(s, i), m_at(p)).start())
+            remote(m_at(c), at(0, c), CROSS, lane_at(s, i), {"pcol": pcol_x}).start()
+
     @pl.when(is_s0)
     def _():
-        def ahead(t, lane, slot):
-            for i in range(SPLIT):
-                p = row_of(t, lane, i)
-                pl.when(far)(lambda: fwd_copy(0, p, lane_at(slot, i), m_at(p)).start())
-
-        def across(t, lane, slot):
-            for i in range(SPLIT):
-                p = row_of(t, lane, i)
-                remote(m_at(p), at(0, p), CROSS, lane_at(slot, i), {"pcol": pcol_x}).start()
-
-        def send(t):
-            ahead(t, 0, t)
-            across(t, 1, t)
-
-        loop(a0, tiles, send)
-        ahead(end, 1, tiles)
-        across(end, 0, tiles)
+        loop(0, RING, push)
 
     @pl.when(is_s1)
     def _():
@@ -265,17 +271,20 @@
         @pl.when(borrows)
         def _():
             def one(k):
+                s = n_ax + EARLY + k
+                pl.when(far)(lambda: gate(s))
                 lend_copy(k).wait_recv()
                 for i in range(SPLIT):
-                    pl.when(far)(lambda: fwd_copy(1, spare_row(k, i), lane_at(k, i)).start())
+                    pl.when(far)(lambda: fwd_copy(1, spare_row(k, i), lane_at(s, i)).start())
 
             loop(0, mine, one)
 
-    def send_lower(t, lane, slot):
-        pl.when(far & ((t == b0) | (t == MID)))(lambda: allowed(Z))
-        for i in range(SPLIT):
-            p = row_of(t, lane, i)
-            pl.when(far & (t >= b0))(lambda: fwd_copy(1, p, lane_at(slot, i)).start())
+    def send_lower(t, lane, s):
+        @pl.when(far)
+        def _():
+            gate(s)
+            for i in range(SPLIT):
+                fwd_copy(1, row_of(t, lane, i), lane_at(s, i)).start()
 
     @pl.when(is_s0)
     def _():
@@ -283,6 +292,7 @@
             t = a0 + i
             here = tile_of(t)
             buf[0, here] = times_upper(buf[0, here], us, 0)
+            pl.when(i == n_a - 2)(lambda: loop(RING, RING + BLOCK, push))
             pl.when(i == jnp.where(prow == 0, HEAD_AT, n_a - 1))(take_head)
 
         loop(0, n_a, low_step)
@@ -292,28 +302,41 @@
             unit_copy(t, lane, slot, own).wait_recv()
             make_lower(t, buf[0, unit_of(t, lane)], lane)
 
-        def send(t):
-            send_lower(t, 0, t)
+        first = PER + 1
+
+        def show(t):
             unit_copy(t, 0, t, buf.at[1]).start()
+
+        def send(k):
+            pl.when(k == EARLY)(borrow)
+            send_lower(b0 + k, 0, step_of(k))
 
         def step(i):
             t = a0 + i
             make(t, 0, t)
             lend(t - 1)
-            pl.when(i == EARLY + 1 + b0 - a0)(borrow)
-            pl.when(i >= 1)(lambda: send(t - 1))
+            pl.when(i >= PER)(lambda: show(t - PER))
+
+            @pl.when(i < PER)
+            def _():
+                for n in range(2):
+                    k = RING + BLOCK + 2 * i + n
+                    pl.when(k <= n_a)(lambda: push(k))
+
+            pl.when(i >= first)(lambda: send(i - first))
 
         loop(0, n_a, step)
         make(end, 1, tiles)
-        send_lower(end, 0, end)
-        send_lower(end, 1, tiles)
+        loop(n_a - first, n_b, send)
+        loop(tiles - PER, end, show)
+        send_lower(end, 1, total - 1)
 
     @pl.when(is_s1)
     def _():
         lag = 8
 
-        def relay(t, i):
-            p, sem = row_of(t, 1, i), lane_at(t, i)
+        def relay(s, i):
+            p, sem = row_of(a0 + s, 1, i), lane_at(s, i)
             arrived(0, p, sem)
             pl.when(far)(lambda: fwd_copy(0, p, sem).start())
 
@@ -336,9 +359,11 @@
         def step(s):
             pl.when(s == jnp.where(r == 0, PER, lag))(take_head)
             pl.when(s == lag)(make_u0)
+            pl.when(far)(lambda: gate(s))
             for i in range(SPLIT):
-                relay(a0 + s, i)
+                relay(s, i)
                 pl.when(s >= lag)(functools.partial(make_part, a0 + s - lag, i))
+            open_gate(s, n_a + 1, X, {"pcol": pcol_x})
 
         loop(0, n_a - 1, step)
 
@@ -348,7 +373,7 @@
 
         def late(i):
             pl.when(i == EARLY)(borrow)
-            send_lower(b0 + i, 1, b0 + i)
+            send_lower(b0 + i, 1, step_of(i))
 
             @pl.when(i <= lag + 1)
             def _():
@@ -357,12 +382,12 @@
                 @pl.when(i >= lag)
                 def _():
                     for n in range(SPLIT):
-                        arrived(0, row_of(end, lane, n), lane_at(tiles - lane, n))
+                        arrived(0, row_of(end, lane, n), lane_at(n_a - lane, n))
 
                 make(jnp.minimum(end - lag + i, end), lane)
 
         loop(0, n_b, late)
-        send_lower(end, 0, tiles)
+        send_lower(end, 0, total - 1)
 
         def finish(t):
             unit_copy(t, 0, t, buf.at[1]).wait_recv()
@@ -372,8 +397,6 @@
     @pl.when(is_g)
     def _():
         lag_a, lag_b = 6, 4
-        n_ax = n_a + 1 - 2 * x
-        total = n_ax + n_r + n_b + 1
         give_from = n_ax + EARLY + 3
         use_lent = tiles - PER + EARLY + jnp.where(r == 0, 9, 14)
         first_of_1 = lag_a + PER
@@ -401,8 +424,7 @@
 
         def apply_b(t, was_lent):
             if was_lent:
-                for i in range(SPLIT):
-                    arrived(1, row_of(t, x, i), lane_at(t, i))
+                give_copy(t).wait_recv()
 
             pl.when(t < end)(lambda: unit_copy(t, 1 - x, t, buf.at[1]).wait_recv())
             here = tile_of(t)
@@ -440,15 +462,15 @@
             @pl.when(in_b & ((k == 0) | (t == MID)))
             def _():
                 allowed(X)
-                pl.when(far)(lambda: allowed(Z))
-
+
+            pl.when(far & (s < total))(lambda: gate(s))
             pl.when(borrows & (s == n_ax + EARLY))(lambda: allowed(Y))
             ta = s - lag_a
 
             def micro(i):
                 @pl.when((s < total) & jnp.logical_not(in_r))
                 def _():
-                    p, sem = row_of(t, lane, i), lane_at(slot, i)
+                    p, sem = row_of(t, lane, i), lane_at(s, i)
                     arrived(ph, p, sem)
                     pl.when(far)(lambda: fwd_copy(ph, p, sem).start())
                     pl.when(in_a | (t < end))(lambda: cross_copy(ph, p, unit_at(slot)).start())
@@ -456,11 +478,11 @@
                 @pl.when(in_r)
                 def _():
                     n = s - n_ax - EARLY
-                    p, sem = spare_row(n, i), lane_at(n, i)
+                    p, sem = spare_row(n, i), lane_at(s, i)
                     arrived(1, p, sem)
                     pl.when(far)(lambda: fwd_copy(1, p, sem).start())
                     cross_copy(1, p, unit_at(n)).start()
-                    give_copy(n, i).start()
+                    pl.when(i == SPLIT - 1)(lambda: give_copy(n).start())
 
                 pl.when((i == 0) & (ta >= 0) & (ta < n_a))(lambda: lower_a(a0 + ta))
                 pl.when((i == 1) & (ta >= 0) & (ta < n_a))(lambda: apply_a(a0 + ta))
@@ -469,7 +491,7 @@
 
             loop(0, SPLIT, micro)
 
-            pl.when((s == MID - 1 - a0) | (s == n_ax - 1))(lambda: allow(Z, {"pcol": pcol - 2}))
+            open_gate(s, total, Z, {"pcol": pcol - 2})
             pl.when((ta == MID - 1 - a0) | (ta == n_a - 1))(lambda: allow(X, {"pcol": pcol_x}))
             pl.when(lends & (ta == MID - 1 - a0))(lambda: allow(Y, {"prow": prow - 2}))
 
@@ -570,7 +592,7 @@
             pltpu.VMEM((2, PIECES) + square, BF),
             pltpu.VMEM(square, BF),
             dma((4,)),
-            dma((SPLIT * (tiles + 1),)),
+            dma((SPLIT * RING,)),
             dma((tiles + 1,)),
             dma((PER,)),
             dma((3,)),

time: 88.7 us -> 88.2 us (level)
  no operation moved by 1% of the time
where the time goes in v8:
time: 88.2 us; the launch traced here: 88 us
  Pallas kernels  88 us (100%)
    pallas_call x1, Pallas kernels, body(): pl.pallas_call(functools.partial(kernel, n_prow, n_pcol, width), out_shap...  86.1 us
    pallas_call x1, Pallas kernels, body(): pl.pallas_call(finish, out_shape=jax.ShapeDtypeStruct(matrix.shape, BF),...  1.87 us

profile of v8, /device:TPU:29, one launch (start us, length us, event | category | flops | bytes accessed | tf_op | source)
XLA Modules:
  0.0 88.0 jit_solution(11410033976123219053)
XLA Ops:
  0.0 86.1 %shard_map.37 = (bf16[3584,512]{1,0:T(8,128)(2,1)S(1)}, bf16[2,4096,512]{2,1,0:T(8,128)(2,1)S(1)}, bf16[512,512]{1,0:T(8,128)(2,1)S(1)}) custom-call(bf16[3584,512]{1,0:T(8,128)(2,1)} %m_ref.1, f32[2,512,512]{2,1,0:T(8,128)} %u_hbm.1, f32[2,512,512]{2,1,0:T(8,128)} %l_hbm.1), custom_call_target="tpu_custom_call" | custom-call | tf_op jit(solution)/shard_map/pallas_call | solution.py:581
  86.1 1.9 %shard_map.38 = bf16[3584,512]{1,0:T(8,128)(2,1)} custom-call(bf16[3584,512]{1,0:T(8,128)(2,1)S(1)} %get-tuple-element.8.own, bf16[2,4096,512]{2,1,0:T(8,128)(2,1)S(1)} %get-tuple-element.9.buf, bf16[512,512]{1,0:T(8,128)(2,1)S(1)} %get-tuple-element.10.u1), custom_call_target="tpu_custom_call" | custom-call | tf_op jit(solution)/shard_map/pallas_call | solution.py:607

commit v9 on v8

--- a/solution.py
+++ b/solution.py
@@ -210,8 +210,8 @@
         t, lane = jnp.where(s < n_a, a0 + s, end), jnp.where(s < n_a, 0, 1)
         for i in range(SPLIT):
             p, c = row_of(t, lane, i), row_of(t, 1 - lane, i)
+            remote(m_at(c), at(0, c), CROSS, lane_at(s, i), {"pcol": pcol_x}).start()
             pl.when(far)(lambda: fwd_copy(0, p, lane_at(s, i), m_at(p)).start())
-            remote(m_at(c), at(0, c), CROSS, lane_at(s, i), {"pcol": pcol_x}).start()
 
     @pl.when(is_s0)
     def _():

time: 88.2 us -> 88.2 us (level)
  no operation moved by 1% of the time
where the time goes in v9:
time: 88.2 us; the launch traced here: 88 us
  Pallas kernels  88 us (100%)
    pallas_call x1, Pallas kernels, body(): pl.pallas_call(functools.partial(kernel, n_prow, n_pcol, width), out_shap...  86.1 us
    pallas_call x1, Pallas kernels, body(): pl.pallas_call(finish, out_shape=jax.ShapeDtypeStruct(matrix.shape, BF),...  1.87 us

profile of v9, /device:TPU:29, one launch (start us, length us, event | category | flops | bytes accessed | tf_op | source)
XLA Modules:
  0.0 88.0 jit_solution(2884793099628758978)
XLA Ops:
  0.0 86.1 %shard_map.37 = (bf16[3584,512]{1,0:T(8,128)(2,1)S(1)}, bf16[2,4096,512]{2,1,0:T(8,128)(2,1)S(1)}, bf16[512,512]{1,0:T(8,128)(2,1)S(1)}) custom-call(bf16[3584,512]{1,0:T(8,128)(2,1)} %m_ref.1, f32[2,512,512]{2,1,0:T(8,128)} %u_hbm.1, f32[2,512,512]{2,1,0:T(8,128)} %l_hbm.1), custom_call_target="tpu_custom_call" | custom-call | tf_op jit(solution)/shard_map/pallas_call | solution.py:581
  86.1 1.9 %shard_map.38 = bf16[3584,512]{1,0:T(8,128)(2,1)} custom-call(bf16[3584,512]{1,0:T(8,128)(2,1)S(1)} %get-tuple-element.8.own, bf16[2,4096,512]{2,1,0:T(8,128)(2,1)S(1)} %get-tuple-element.9.buf, bf16[512,512]{1,0:T(8,128)(2,1)S(1)} %get-tuple-element.10.u1), custom_call_target="tpu_custom_call" | custom-call | tf_op jit(solution)/shard_map/pallas_call | solution.py:607
